TPU v7x, 512 devices: a whole 4x4x16 slice. The times are simulated.
512 devices in a mesh: visit: 64 (over z, y), template: 8 (over x, core).
Axes of the slice: x: 4, y: 4, z: 16, core: 2. Of those that a mesh axis runs over, the one named last changes fastest.
Arguments:
- template: bfloat16 [64, 256, 1152], P('visit', 'template'), may hold values from -5 to 5
- science: bfloat16 [384, 4, 256, 128], P('visit', None, 'template'), may hold values from -27 to 27
- variance: bfloat16 [384, 4, 256, 128], P('visit', None, 'template'), may hold values from 0.5 to 2
- bad_pixels: int32 [384, 4, 256, 128], P('visit', None, 'template'), may hold values 0 or 1
- intersection_patch: int32 [384, 4], P('visit'), may hold values from 0 to 63, as said below
- intersection_block: int32 [384, 4], P('visit'), may hold values from 0 to 7
Outputs:
- significance: float32 [64, 256, 1024], P('visit', 'template')
Inputs may be any that keep to these rules, and one draw needn't show every extreme that they name: `intersection_patch`: each visit's 4 patches are different. Among the 6 visits of one index of visit (an aligned block of rows), every patch that is named is named exactly 2 times, and one patch is named 2 times in every such block.
All inputs are finite; a program needn't handle non-finite values. No bound on the sum of `bad_pixels` on one device may be relied on, other than what follows from the above.
Results may differ from a plain program's by a relative error of at most 0.0032.
Values may be sent and summed in bfloat16 or wider, within the bound.
A program may use at most 128 MiB of HBM per device.

v0:
```python
import jax
import jax.numpy as jnp
from jax import lax
from jax.sharding import PartitionSpec as P

NBLK = 8
MARGIN = 64
HALF = 10


RIDGE = 0.05


def extended(value, sides, width):
    for axis, dim in sides:
        size, length = (lax.axis_size(axis), value.shape[dim])
        up = [(i, (i + 1) % size) for i in range(size - 1)]
        down = [(j, i) for i, j in up]
        last = lax.slice_in_dim(value, length - width, length, axis=dim)
        leading = lax.slice_in_dim(value, 0, width, axis=dim)
        before = lax.ppermute(last, axis, up)
        after = lax.ppermute(leading, axis, down)
        value = jnp.concatenate([before, value, after], axis=dim)
    return value


def basis_taps():
    spread = jnp.arange(2 * HALF + 1, dtype=jnp.float32)
    scaled = (HALF - spread) / 2.5
    hermite = jnp.stack(
        [
            jnp.ones(scaled.shape, jnp.float32),
            2.0 * scaled,
            4.0 * scaled * scaled - 2.0,
            8.0 * scaled * scaled * scaled - 12.0 * scaled,
        ]
    )
    shaped = hermite * jnp.exp(-0.5 * scaled * scaled)
    shaped = shaped / jnp.sqrt(jnp.sum(shaped * shaped, axis=1, keepdims=True))
    return shaped.astype(jnp.bfloat16)


def solve_normal(system):
    unknowns = system.shape[0]
    rows_index = jnp.arange(unknowns)[:, None, None]
    for column in range(unknowns):
        pivot_row = system[column] / system[column, column][None, :]
        factor = system[:, column, :]
        updated = system - factor[:, None, :] * pivot_row[None, :, :]
        system = jnp.where(rows_index == column, pivot_row[None, :, :], updated)
    return system[:, unknowns, :]


def column_table(profile, block_span, block_width):
    offsets = jnp.arange(block_span)[:, None] - jnp.arange(block_width)[None, :] - (MARGIN - HALF)
    choose = (offsets[None] == jnp.arange(2 * HALF + 1)[:, None, None]).astype(jnp.float32)
    toeplitz = jnp.einsum("at,tnc->nac", profile.astype(jnp.float32), choose)
    return toeplitz.reshape(block_span, 4 * block_width).astype(jnp.bfloat16)


def row_table(profile, strip_rows):
    offsets = jnp.arange(strip_rows + 2 * HALF)[None, :] - jnp.arange(strip_rows)[:, None]
    choose = (offsets[None] == jnp.arange(2 * HALF + 1)[:, None, None]).astype(jnp.float32)
    toeplitz = jnp.einsum("bt,trm->brm", profile.astype(jnp.float32), choose)
    return toeplitz.reshape(4 * strip_rows, strip_rows + 2 * HALF).astype(jnp.bfloat16)


def body(template, science, variance, bad_pixels, intersection_patch, intersection_block):
    profile = basis_taps()
    visit_count, block_count, strip_rows, block_width = science.shape
    device_count = lax.axis_size("visit")
    own_index = lax.axis_index("visit")
    slot_count = visit_count * block_count
    capacity = max(2, -(-slot_count // device_count))
    block_span = block_width + 2 * MARGIN
    padded_rows = strip_rows + 2 * HALF
    all_patch, all_block = (
        lax.all_gather(intersection_patch, "visit", axis=0, tiled=True),
        lax.all_gather(intersection_block, "visit", axis=0, tiled=True),
    )
    source_patch = all_patch.reshape(device_count, slot_count)
    source_block = all_block.reshape(device_count, slot_count)
    slot_index = jnp.arange(slot_count)
    earlier = slot_index[None, :] < slot_index[:, None]
    same_patch = source_patch[:, :, None] == source_patch[:, None, :]
    source_rank = jnp.sum(same_patch & earlier[None], axis=2)
    own_patch = intersection_patch.reshape(slot_count)
    own_rank = lax.dynamic_index_in_dim(source_rank, own_index, 0, keepdims=False)
    own_slot = own_patch * capacity + own_rank
    wanted = (source_patch == own_index)[:, None, :] & (
        source_rank[:, None, :] == jnp.arange(capacity)[None, :, None]
    )
    at_block = source_block[:, :, None] == jnp.arange(NBLK)[None, None, :]
    chooser = jnp.einsum(
        "uck,uko->uco", wanted.astype(jnp.float32), at_block.astype(jnp.float32)
    ).astype(jnp.bfloat16)
    rimmed_strip = extended(template[0], (("template", 0),), HALF)
    strips = lax.all_gather(rimmed_strip[None], "visit", axis=0, tiled=True)
    own_block = intersection_block.reshape(slot_count)

    def cut_block(patch_id, column_block):
        return lax.dynamic_slice(
            strips, (patch_id, 0, column_block * block_width), (1, padded_rows, block_span)
        )[0]

    gathered_blocks = jax.vmap(cut_block)(own_patch, own_block)
    gathered_blocks = gathered_blocks.reshape(visit_count, block_count, padded_rows, block_span)
    across = column_table(profile, block_span, block_width)
    vertical = row_table(profile, strip_rows)
    usable = (1 - bad_pixels).astype(jnp.bfloat16)

    def convolve(inputs):
        blocks, signal, usable_mask = inputs
        smooth = jnp.einsum(
            "jmn,nx->jmx", blocks, across, preferred_element_type=jnp.float32
        ).astype(jnp.bfloat16)
        images = jnp.einsum(
            "ym,jmx->jyx", vertical, smooth, preferred_element_type=jnp.float32
        ).astype(jnp.bfloat16)
        basis_images = images.reshape(block_count, 4, strip_rows, 4, block_width)
        weighted = basis_images * usable_mask[:, None, :, None, :]
        cross_terms = jnp.einsum(
            "jbrac,jdrec->bade", weighted, basis_images, preferred_element_type=jnp.float32
        ).reshape(16, 16)
        with_ones = jnp.einsum(
            "jbrac,jrc->ba", basis_images, usable_mask, preferred_element_type=jnp.float32
        ).reshape(16)
        masked_signal = signal * usable_mask
        with_signal = jnp.einsum(
            "jbrac,jrc->ba", basis_images, masked_signal, preferred_element_type=jnp.float32
        ).reshape(16)
        usable_total = jnp.sum(usable_mask.astype(jnp.float32))
        signal_total = jnp.sum(masked_signal.astype(jnp.float32))
        upper_rows = jnp.concatenate(
            [cross_terms, with_ones[:, None], with_signal[:, None]], axis=1
        )
        bottom = jnp.concatenate([with_ones, usable_total[None], signal_total[None]])[None]
        return (images, jnp.concatenate([upper_rows, bottom], axis=0))

    images_all, partial_sums = lax.map(convolve, (gathered_blocks, science, usable))
    normal = lax.psum(partial_sums, "template")
    ridge_term = RIDGE * (normal[:, 16, 16] + 1.0)
    system = normal + ridge_term[:, None, None] * jnp.eye(17, 18, dtype=jnp.float32)[None]
    fitted = solve_normal(jnp.transpose(system, (1, 2, 0)))

    def differ(inputs):
        images, signal, noise_var, usable_mask, fit_row = inputs
        basis_images = images.reshape(block_count, 4, strip_rows, 4, block_width).astype(
            jnp.float32
        )
        modeled = (
            jnp.einsum(
                "jbrac,ba->jrc",
                basis_images,
                fit_row[:16].reshape(4, 4),
                precision=lax.Precision.HIGHEST,
            )
            + fit_row[16]
        )
        difference = signal.astype(jnp.float32) - modeled
        weight = usable_mask.astype(jnp.float32) / noise_var.astype(jnp.float32)
        return jnp.stack(
            [(weight * difference).astype(jnp.bfloat16), weight.astype(jnp.bfloat16)], axis=1
        )

    payload = lax.map(differ, (images_all, science, variance, usable, fitted.T))
    payload = payload.reshape(slot_count, 2 * strip_rows * block_width)
    placement = (own_slot[None, :] == jnp.arange(device_count * capacity)[:, None]).astype(
        jnp.bfloat16
    )
    outgoing = jnp.einsum(
        "sk,kx->sx", placement, payload, preferred_element_type=jnp.float32
    ).astype(jnp.bfloat16)
    outgoing = outgoing.reshape(device_count, capacity, 2, strip_rows, block_width)
    incoming = lax.all_to_all(outgoing, "visit", split_axis=0, concat_axis=0, tiled=True)
    accumulated = jnp.einsum(
        "uco,ucqrx->oqrx", chooser, incoming, preferred_element_type=jnp.float32
    )
    significance = accumulated[:, 0] / jnp.sqrt(jnp.maximum(accumulated[:, 1], 1.0))
    return significance.transpose(1, 0, 2).reshape(1, strip_rows, NBLK * block_width)


def solution(mesh):
    return jax.shard_map(
        body,
        mesh=mesh,
        in_specs=(
            P("visit", "template", None),
            P("visit", None, "template", None),
            P("visit", None, "template", None),
            P("visit", None, "template", None),
            P("visit", None),
            P("visit", None),
        ),
        out_specs=P("visit", "template", None),
        check_vma=False,
    )
```

profile of v0, /device:TPU:24, one launch (start us, length us, event | category | flops | bytes accessed | tf_op | source)
XLA Modules:
  0.0 546.1 jit_solution(14429271509945404964)
XLA Ops:
  6.5 0.8 slice_bitcast_fusion.1
  7.4 1.7 collective-permute-start
  9.1 1.3 collective-permute-start.1
  10.4 3.1 collective-permute-done.1
  13.5 1.6 maximum_bitcast_fusion.3
  18.3 105.9 %all-gather.1 = s32[64,6,4]{1,2,0:T(4,128)S(1)} all-gather(s32[1,6,4]{1,2,0:T(4,128)} %bitcast.457), channel_id=1, replica_groups=mesh['visit'=64,'template'=8] {'visit'}, dimensions={0}, use_global_device_ids=true | all-gather | bytes 6240 | tf_op jit(solution)/shard_map/all_gather | solution.py:78
  125.8 49.5 %all-gather.6.cloned.1.call-done = bf16[64,52,1152]{2,1,0:T(8,128)(2,1)} async-done(((bf16[1,52,1152]{2,1,0:T(8,128)(2,1)}), bf16[64,52,1152]{2,1,0:T(8,128)(2,1)}) %all-gather.6.cloned.1.call-update) | async-done | bytes 7667728 | tf_op jit(solution)/shard_map/all_gather | solution.py:98
  175.3 29.8 %copy.313 = bf16[64,52,1152]{1,0,2:T(8,128)(2,1)} copy(bf16[64,52,1152]{2,1,0:T(8,128)(2,1)} %all-gather.6.cloned.1.call-done) | data formatting | bytes 15335424 | tf_op jit(solution)/shard_map/all_gather | solution.py:98
  205.1 8.5 %gather_fusion = bf16[24,52,256]{1,0,2:T(8,128)(2,1)S(1)} fusion(bf16[64,52,1152]{1,0,2:T(8,128)(2,1)} %copy.313, s32[24]{0:T(128)S(1)} %fusion.71), kind=kCustom, calls=%fused_computation | custom fusion | bytes 1278240 | tf_op jit(solution)/shard_map/vmap()/gather | solution.py:102
  213.6 1.2 copy.315
  214.9 49.1 %while.22 = (s32[]{:T(128)}, bf16[6,4,128,512]{2,3,1,0:T(8,128)(2,1)}, f32[6,17,18]{2,0,1:T(8,128)S(1)}, bf16[6,4,52,256]{3,2,1,0:T(8,128)(2,1)S(1)}, bf16[256,5...) while((s32[]{:T(128)}, ...), condition=%wide.region_5.6_spmd, body=%wide.region_2.5_spmd.sunk | while | flops 91956152 | bytes 9150269 | solution.py:140
  214.9 1.4 bitcast_dynamic-update-slice_fusion.2
  216.6 2.4 fusion.105
  219.8 1.4 maximum_bitcast_fusion.6
  223.1 1.3 bitcast_dynamic-update-slice_fusion.2
  224.8 2.4 fusion.105
  228.0 1.4 maximum_bitcast_fusion.6
  231.3 1.3 bitcast_dynamic-update-slice_fusion.2
  233.0 2.4 fusion.105
  236.2 1.4 maximum_bitcast_fusion.6
  239.4 1.3 bitcast_dynamic-update-slice_fusion.2
  241.1 2.4 fusion.105
  244.3 1.4 maximum_bitcast_fusion.6
  247.6 1.4 bitcast_dynamic-update-slice_fusion.2
  249.3 2.4 fusion.105
  252.5 1.4 maximum_bitcast_fusion.6
  255.8 1.4 bitcast_dynamic-update-slice_fusion.2
  257.6 2.4 fusion.105
  260.8 1.4 maximum_bitcast_fusion.6
  264.0 24.5 %psum.7 = f32[6,17,18]{2,0,1:T(8,128)S(1)} all-reduce(f32[6,17,18]{2,0,1:T(8,128)S(1)} %get-tuple-element.86), channel_id=1, replica_groups=mesh['visit'=64,'template'=8] {'template'}, use_global_device_ids=true, to_apply=%region_6.7 | all-reduce | flops 1836 | bytes 14688 | tf_op jit(solution)/shard_map/psum | solution.py:141
  305.3 30.3 %while.23 = (s32[]{:T(128)}, bf16[6,4,2,32,128]{4,3,2,1,0:T(8,128)(2,1)S(1)}, bf16[6,4,32,128]{3,2,1,0:T(8,128)(2,1)S(1)}, bf16[6,4,32,128]{3,2,1,0:T(8,128)(2,1...) while((s32[]{:T(128)}, ...), condition=%wide.region_8.9_spmd, body=%wide.region_7.8_spmd.sunk | while | flops 3473410 | bytes 4162109 | solution.py:166
  305.4 1.1 constant_dynamic-slice_fusion.4
  308.1 1.4 fusion.109
  310.5 1.1 constant_dynamic-slice_fusion.4
  313.1 1.4 fusion.109
  314.5 0.8 convert_bitcast_fusion.2
  315.5 1.1 constant_dynamic-slice_fusion.4
  318.1 1.4 fusion.109
  320.5 1.1 constant_dynamic-slice_fusion.4
  323.1 1.4 fusion.109
  325.5 1.1 constant_dynamic-slice_fusion.4
  328.2 1.4 fusion.109
  330.5 1.1 constant_dynamic-slice_fusion.4
  333.2 1.4 fusion.109
  337.1 5.2 copy.354
  342.4 11.4 %all-to-all-start = ((bf16[64,2,2,32,128]{4,1,3,2,0:T(2,128)(2,1)}), bf16[64,2,2,32,128]{4,1,3,2,0:T(2,128)(2,1)S(1)}, u32[]{:S(2)}, u32[]{:S(2)}) async-start(bf16[64,2,2,32,128]{4,1,3,2,0:T(2,128)(2,1)} %copy.354), calls=%async_computation | async-start | bytes 4194304 | tf_op jit(solution)/shard_map/all_to_all | solution.py:175
  354.0 181.8 %all-gather.2 = s32[64,6,4]{1,2,0:T(4,128)S(1)} all-gather(s32[1,6,4]{1,2,0:T(4,128)S(1)} %bitcast.458), channel_id=1, replica_groups=mesh['visit'=64,'template'=8] {'visit'}, dimensions={0}, use_global_device_ids=true | all-gather | bytes 6240 | tf_op jit(solution)/shard_map/all_gather | solution.py:79
  536.2 2.3 fusion.26
  (300 shorter events, 55.7 us)
Async XLA Ops:
  6.5 119.2 %copy-start.1 = (s32[6,4,32,128]{3,2,1,0:T(8,128)S(1)}, s32[6,4,32,128]{3,2,1,0:T(8,128)}, u32[]{:S(2)}) copy-start(s32[6,4,32,128]{3,2,1,0:T(8,128)} %param.13) | copy-start | bytes 1179652
  6.5 168.7 %all-gather.6.cloned.1.call-start = ((), (), s32[]{:S(2)}) async-start(), calls=%async_computation.1 | async-start | bytes 8386560 | tf_op jit(solution)/shard_map/all_gather | solution.py:98
  7.4 3.1 collective-permute-start
  9.1 4.4 collective-permute-start.1
  205.1 9.8 %copy-start = (bf16[6,4,32,128]{3,2,1,0:T(8,128)(2,1)S(1)}, bf16[6,4,32,128]{3,2,1,0:T(8,128)(2,1)}, u32[]{:S(2)}) copy-start(bf16[6,4,32,128]{3,2,1,0:T(8,128)(2,1)} %param.11) | copy-start | bytes 589828
  342.4 11.6 %copy-start.2 = (s32[6,4]{0,1:T(4,128)S(1)}, s32[6,4]{0,1:T(4,128)}, u32[]{:S(2)}) copy-start(s32[6,4]{0,1:T(4,128)} %param.15) | copy-start | bytes 292
  342.4 193.8 %all-to-all-start = ((bf16[64,2,2,32,128]{4,1,3,2,0:T(2,128)(2,1)}), bf16[64,2,2,32,128]{4,1,3,2,0:T(2,128)(2,1)S(1)}, u32[]{:S(2)}, u32[]{:S(2)}) async-start(bf16[64,2,2,32,128]{4,1,3,2,0:T(2,128)(2,1)} %copy.354), calls=%async_computation | async-start | bytes 4194304 | tf_op jit(solution)/shard_map/all_to_all | solution.py:175
Sparse Core Ops, SparseCore 0:
  15.2 159.9 all-gather.5
where the time goes:
time: 549 us; the launch traced here: 546 us
  blocking collectives  312 us (57%)
  local copies, waits for them, and re-layouts  75.3 us (14%)
  waiting for transfers between devices  52.6 us (10%)
  other arithmetic  39.7 us (7%)
  matrix products  36.9 us (7%)
  starting transfers between devices  14.4 us (3%)
  between operations  13.9 us (3%)
    all_gather x1, blocking collectives, body(): lax.all_gather(intersection_block, 'visit', axis=0, tiled=True)  182 us
    all_gather x1, blocking collectives, body(): lax.all_gather(intersection_patch, 'visit', axis=0, tiled=True)  106 us
    all_gather x1, waiting for transfers between devices, body(): strips = lax.all_gather(rimmed_strip[None], 'visit', axis=0, tiled=True)  49.5 us
    all_gather x1, local copies, waits for them, and re-layouts, body(): strips = lax.all_gather(rimmed_strip[None], 'visit', axis=0, tiled=True)  29.8 us
    psum x1, blocking collectives, body(): normal = lax.psum(partial_sums, 'template')  24.5 us
    dot_general x6, matrix products, convolve(): jnp.einsum('jbrac,jrc->ba', basis_images, usable_mask, preferred_element_...  14.3 us
    all_to_all x1, starting transfers between devices, body(): lax.all_to_all(outgoing, 'visit', split_axis=0, concat_axis=0, tiled=True)  11.4 us
  transfers between devices with their start and end apart: 4, of which 2 were waited for; matrix products, arithmetic and copies ran while one was open for 1% of the time, Pallas kernels for 0%

commit v1 on v0

v1 whole, which is shorter than its diff:
```python
import functools

import jax
import jax.numpy as jnp
import numpy as np
from jax import lax
from jax.experimental import pallas as pl
from jax.experimental.pallas import tpu as pltpu
from jax.sharding import PartitionSpec as P

NBLK = 8
MARGIN = 64
HALF = 10
RIDGE = 0.05
NZ, NY = 16, 4
NDEV = NZ * NY
NTEM = 8
MESH = pl.DeviceIdType.MESH
F32 = jnp.float32
BF16 = jnp.bfloat16


def basis_taps():
    spread = jnp.arange(2 * HALF + 1, dtype=jnp.float32)
    scaled = (HALF - spread) / 2.5
    hermite = jnp.stack(
        [
            jnp.ones(scaled.shape, jnp.float32),
            2.0 * scaled,
            4.0 * scaled * scaled - 2.0,
            8.0 * scaled * scaled * scaled - 12.0 * scaled,
        ]
    )
    shaped = hermite * jnp.exp(-0.5 * scaled * scaled)
    shaped = shaped / jnp.sqrt(jnp.sum(shaped * shaped, axis=1, keepdims=True))
    return shaped.astype(jnp.bfloat16)


def tables():
    profile = np.asarray(basis_taps().astype(jnp.float32))
    across = np.zeros((256, 4, 128), np.float32)
    vertical = np.zeros((4, 32, 64), np.float32)
    for t in range(2 * HALF + 1):
        for c in range(128):
            across[c + t + MARGIN - HALF, :, c] = profile[:, t]
        for r in range(32):
            vertical[:, r, r + t + 16 - HALF] = profile[:, t]
    return across.reshape(256, 512), vertical.reshape(128, 64)


def wrap(value, size):
    return lax.rem(value + size, size)


def gather_kernel(strip, ids, got, got_ids, send_sem, id_send, ay, az, bz, by, iy, iz):
    me = lax.axis_index("visit")
    tem = lax.axis_index("template")
    z, y = lax.div(me, NY), lax.rem(me, NY)

    def at(dz, dy):
        return (wrap(z + dz, NZ) * NY + wrap(y + dy, NY), tem)

    barrier = pltpu.get_barrier_semaphore()
    partners = [at(0, 1), at(0, -1), at(0, 2), at(1, 0), at(-1, 0)]
    for partner in partners:
        pl.semaphore_signal(barrier, inc=1, device_id=partner, device_id_type=MESH)
    pl.semaphore_wait(barrier, len(partners))

    def send(src, dst, sem, recv, target):
        pltpu.make_async_remote_copy(
            src_ref=src, dst_ref=dst, send_sem=sem, recv_sem=recv,
            device_id=target, device_id_type=MESH,
        ).start()

    def arrive(dst, recv):
        pltpu.make_async_copy(dst, dst, recv).wait()

    def slot(zz, yy):
        return wrap(zz, NZ) * NY + wrap(yy, NY)

    def a_ref(zz, yy):
        return got.at[0, slot(zz, yy)]

    def b_ref(zz, yy):
        return got.at[1, slot(zz, yy)]

    for d in (1, 3, 2):
        dy = {1: 1, 2: 2, 3: -1}[d]
        send(ids, got_ids.at[me], id_send, iy.at[d - 1], at(0, dy))
        send(strip.at[0], a_ref(z, y), send_sem, ay.at[d - 1], at(0, dy))
    for k, dz in ((0, 1), (1, -1)):
        send(strip.at[1], b_ref(z, y), send_sem, bz.at[k, 0], at(dz, 0))
        send(strip.at[0], a_ref(z, y), send_sem, az.at[k, 0, 0], at(dz, 0))
    for k, dy in ((0, 1), (1, -1)):
        send(strip.at[1], b_ref(z, y), send_sem, by.at[k, 0], at(0, dy))
    got[0, me] = strip[0]
    got[1, me] = strip[1]
    got_ids[me] = ids[...]
    for d in (1, 3, 2):
        dy = {1: 1, 2: 2, 3: -1}[d]
        arrive(a_ref(z, y - dy), ay.at[d - 1])
        for k, dz in ((0, 1), (1, -1)):
            send(a_ref(z, y - dy), a_ref(z, y - dy), send_sem, az.at[k, 0, d], at(dz, 0))
    for d in (1, 3, 2):
        dy = {1: 1, 2: 2, 3: -1}[d]
        arrive(got_ids.at[slot(z, y - dy)], iy.at[d - 1])
    row = got_ids.at[pl.ds(z * NY, NY)]
    for k, dz in ((0, 1), (1, -1)):
        send(row, row, id_send, iz.at[k, 0], at(dz, 0))

    def relay(source, index):
        k = index % 2
        dy = (1, -1)[k]
        arrive(b_ref(source, y - dy), by.at[k, index])
        send(b_ref(source, y - dy), b_ref(source, y - dy), send_sem, by.at[2, index], at(0, dy))

    half_ring = NZ // 2
    relay(z, 0)
    for s in range(1, half_ring + 1):
        for k, dz in ((0, 1), (1, -1)):
            last = s == half_ring
            if last and k == 1:
                continue
            source = z - dz * s
            index = 2 * s - 1 + k
            arrive(b_ref(source, y), bz.at[k, s - 1])
            if s < half_ring - k:
                send(b_ref(source, y), b_ref(source, y), send_sem, bz.at[k, s], at(dz, 0))
            for q, dy in ((0, 1), (1, -1)):
                send(b_ref(source, y), b_ref(source, y), send_sem, by.at[q, index], at(0, dy))
        for d in (0, 1, 3, 2):
            for k, dz in ((0, 1), (1, -1)):
                dy = {0: 0, 1: 1, 2: 2, 3: -1}[d]
                source = z - dz * s
                if s == half_ring and k != (d >= 2):
                    continue
                arrive(a_ref(source, y - dy), az.at[k, s - 1, d])
                if s < half_ring - 1 or (s == half_ring - 1 and k == (d >= 2)):
                    ref = a_ref(source, y - dy)
                    send(ref, ref, send_sem, az.at[k, s, d], at(dz, 0))
        for k, dz in ((0, 1), (1, -1)):
            if s == half_ring and k == 1:
                continue
            source = z - dz * s
            ref = got_ids.at[pl.ds(wrap(source, NZ) * NY, NY)]
            arrive(ref, iz.at[k, s - 1])
            if s < half_ring - k:
                send(ref, ref, id_send, iz.at[k, s], at(dz, 0))
        for k, dz in ((0, 1), (1, -1)):
            if s == half_ring and k == 1:
                continue
            relay(z - dz * s, 2 * s - 1 + k)
    for index in range(NZ):
        s = (index + 1) // 2
        source = z if index == 0 else (z - s if index % 2 == 1 else z + s)
        k = index % 2
        dy = (1, -1)[k]
        arrive(b_ref(source, y + dy), by.at[1 - k, index])
        arrive(b_ref(source, y + 2), by.at[2, index])
    sent = got.at[:, pl.ds(0, NDEV - 1)]
    arrive(sent, send_sem)
    arrive(got_ids.at[pl.ds(0, NDEV - 1)], id_send)


def gather(strip, ids):
    vmem = pl.BlockSpec(memory_space=pltpu.VMEM)
    dma = pltpu.SemaphoreType.DMA
    return pl.pallas_call(
        gather_kernel,
        out_shape=(
            jax.ShapeDtypeStruct((2, NDEV, 16, strip.shape[-1]), BF16),
            jax.ShapeDtypeStruct((NDEV, 1, 128), jnp.int32),
        ),
        in_specs=[vmem, vmem],
        out_specs=(vmem, vmem),
        scratch_shapes=[
            dma, dma, dma((3,)), dma((2, 8, 4)), dma((2, 8)), dma((3, NZ)), dma((3,)), dma((2, 8)),
        ],
        compiler_params=pltpu.CompilerParams(collective_id=0, has_side_effects=True),
    )(strip, ids)


def cut_kernel(patch, block, got, cut, sem):
    for k in range(24):
        first = pl.multiple_of(block[k] * 128, 128)
        for h in range(2):
            pltpu.make_async_copy(
                got.at[h, patch[k], :, pl.ds(first, 256)], cut.at[h, k], sem
            ).start()
    pltpu.make_async_copy(cut, cut, sem).wait()


def cut_blocks(patch, block, got):
    smem = pl.BlockSpec(memory_space=pltpu.SMEM)
    return pl.pallas_call(
        cut_kernel,
        out_shape=jax.ShapeDtypeStruct((2, 24, 16, 256), BF16),
        in_specs=[smem, smem, pl.BlockSpec(memory_space=pl.ANY)],
        out_specs=pl.BlockSpec(memory_space=pltpu.VMEM),
        scratch_shapes=[pltpu.SemaphoreType.DMA],
    )(patch, block, got)


def fit_kernel(
    core, science, variance, bad, across, vertical, payload,
    rim, smooth, images, part, parts, rows, coef, packed, halo_send, halo_recv, sum_send, sum_recv,
):
    me = lax.axis_index("visit")
    tem = lax.axis_index("template")
    visits = science.shape[0]

    barrier = pltpu.get_barrier_semaphore()
    for d in range(1, NTEM):
        pl.semaphore_signal(
            barrier, inc=1, device_id=(me, wrap(tem + d, NTEM)), device_id_type=MESH
        )
    pl.semaphore_wait(barrier, NTEM - 1)

    def halo(source, dest, step, k):
        return pltpu.make_async_remote_copy(
            src_ref=core.at[source], dst_ref=rim.at[dest],
            send_sem=halo_send.at[k], recv_sem=halo_recv.at[k],
            device_id=(me, wrap(tem + step, NTEM)), device_id_type=MESH,
        )

    down, up = halo(1, 0, 1, 0), halo(0, 1, -1, 1)

    @pl.when(tem < NTEM - 1)
    def _():
        down.start()

    @pl.when(tem > 0)
    def _():
        up.start()

    def smear(piece, source):
        result = jnp.dot(
            source.reshape(24 * 16, 256), across[...], preferred_element_type=F32
        )
        smooth[:, piece * 16 : piece * 16 + 16, :] = result.astype(BF16).reshape(24, 16, 512)

    smear(1, core[0])
    smear(2, core[1])

    @pl.when(tem == 0)
    def _():
        rim[0] = jnp.zeros((24, 16, 256), BF16)

    @pl.when(tem == NTEM - 1)
    def _():
        rim[1] = jnp.zeros((24, 16, 256), BF16)

    @pl.when(tem > 0)
    def _():
        down.wait_recv()

    smear(0, rim[0])

    @pl.when(tem < NTEM - 1)
    def _():
        up.wait_recv()

    smear(3, rim[1])

    part[...] = jnp.zeros((24, 128), F32)
    row_id = lax.broadcasted_iota(jnp.int32, (544, 576), 0) & 31
    lane_id = lax.broadcasted_iota(jnp.int32, (544, 576), 1) & 31
    same_row = row_id == lane_id
    pick_row = lax.broadcasted_iota(jnp.int32, (576, 128), 0) >> 5
    pick_lane = lax.broadcasted_iota(jnp.int32, (576, 128), 1)

    def gram(v, carry):
        for j in range(4):
            image = jnp.dot(
                vertical[...], smooth[v * 4 + j], preferred_element_type=F32
            ).astype(BF16)
            for a in range(4):
                images[v, a * 128 : a * 128 + 128, j * 128 : j * 128 + 128] = image[
                    :, a * 128 : a * 128 + 128
                ]
        usable = jnp.concatenate(
            [(1 - bad[v, j]).astype(F32).astype(BF16) for j in range(4)], axis=1
        )
        signal = jnp.concatenate([science[v, j] for j in range(4)], axis=1)
        left = images[v]
        right = jnp.concatenate(
            [left * jnp.concatenate([usable] * 16, axis=0), usable, usable * signal], axis=0
        )
        left = jnp.concatenate([left, usable], axis=0)
        full = lax.dot_general(
            left, right, (((1,), (1,)), ((), ())), preferred_element_type=F32
        )
        full = jnp.where(same_row, full, 0.0)
        sums = jnp.sum(full.reshape(17, 32, 576), axis=1)
        pick = (pick_lane == pick_row + v * 20).astype(F32)
        part[0:17, :] += jnp.dot(
            sums, pick, preferred_element_type=F32, precision=lax.Precision.HIGHEST
        )
        return carry

    lax.fori_loop(0, visits, gram, 0)

    def share(d):
        return pltpu.make_async_remote_copy(
            src_ref=part, dst_ref=parts.at[tem],
            send_sem=sum_send, recv_sem=sum_recv,
            device_id=(me, wrap(tem + d, NTEM)), device_id_type=MESH,
        )

    for d in range(1, NTEM):
        share(d).start()
    parts[tem] = part[...]
    seven = parts.at[pl.ds(0, NTEM - 1)]
    pltpu.make_async_copy(seven, seven, sum_recv).wait()
    total = parts[0]
    for d in range(1, NTEM):
        total = total + parts[d]

    rows[...] = jnp.zeros((192, 128), F32)
    for v in range(visits):
        moved = total if v == 0 else pltpu.roll(total, 128 - 20 * v, 1)
        rows[pl.ds(v, 24, stride=8), :] = moved
    lane = lax.broadcasted_iota(jnp.int32, (8, 128), 1)
    system = [rows[k * 8 : k * 8 + 8, :] for k in range(17)]
    ridge = RIDGE * (system[16][:, 16:17] + 1.0)
    system = [jnp.where(lane == k, system[k] + ridge, system[k]) for k in range(17)]
    for c in range(17):
        pivot = system[c] / system[c][:, c : c + 1]
        system = [
            pivot if k == c else system[k] - system[k][:, c : c + 1] * pivot for k in range(17)
        ]
    for k in range(17):
        coef[k] = jnp.broadcast_to(system[k][:, 17:18], (8, 128))

    low = lax.broadcasted_iota(jnp.int32, (32, 128), 1) < 64

    def differ(v, carry):
        factors = [
            jnp.broadcast_to(coef[k, pl.ds(v, 1), :], (32, 128)) for k in range(17)
        ]
        for j in range(4):
            model = factors[16]
            for k in range(16):
                model = model + factors[k] * images[
                    v, k * 32 : k * 32 + 32, j * 128 : j * 128 + 128
                ].astype(F32)
            difference = science[v, j].astype(F32) - model
            weight = (1 - bad[v, j]).astype(F32) / variance[v, j].astype(F32)
            number = weight * difference
            first = jnp.where(low, number, pltpu.roll(weight, 64, 1))
            second = jnp.where(low, pltpu.roll(number, 64, 1), weight)
            packed[pl.ds(v * 4 + j, 32, stride=24), :] = first
            packed[pl.ds(768 + v * 4 + j, 32, stride=24), :] = second
        return carry

    lax.fori_loop(0, visits, differ, 0)
    payload[...] = packed[...].reshape(NDEV, 3, 8, 128).astype(BF16)

    @pl.when(tem < NTEM - 1)
    def _():
        down.wait_send()

    @pl.when(tem > 0)
    def _():
        up.wait_send()

    pltpu.make_async_copy(seven, seven, sum_send).wait()


def fit(core, science, variance, bad, across, vertical):
    vmem = pl.BlockSpec(memory_space=pltpu.VMEM)
    dma = pltpu.SemaphoreType.DMA
    return pl.pallas_call(
        fit_kernel,
        out_shape=jax.ShapeDtypeStruct((NDEV, 3, 8, 128), BF16),
        in_specs=[vmem] * 6,
        out_specs=vmem,
        scratch_shapes=[
            pltpu.VMEM((2, 24, 16, 256), BF16),
            pltpu.VMEM((24, 64, 512), BF16),
            pltpu.VMEM((6, 512, 512), BF16),
            pltpu.VMEM((24, 128), F32),
            pltpu.VMEM((NTEM, 24, 128), F32),
            pltpu.VMEM((192, 128), F32),
            pltpu.VMEM((17, 8, 128), F32),
            pltpu.VMEM((1536, 128), F32),
            dma((2,)), dma((2,)), dma, dma,
        ],
        compiler_params=pltpu.CompilerParams(collective_id=1, has_side_effects=True),
    )(core, science, variance, bad, across, vertical)


def return_kernel(target, payload, out, inbox, result, final, send1, recv1, send2, recv2):
    me = lax.axis_index("visit")
    tem = lax.axis_index("template")

    def peer(s):
        return lax.rem(me + s, NDEV)

    barrier = pltpu.get_barrier_semaphore()

    def greet(s, carry):
        pl.semaphore_signal(barrier, inc=1, device_id=(peer(s), tem), device_id_type=MESH)
        return carry

    lax.fori_loop(1, NDEV, greet, 0)
    pl.semaphore_wait(barrier, NDEV - 1)

    def push(s, carry):
        pltpu.make_async_remote_copy(
            src_ref=payload.at[peer(s)], dst_ref=inbox.at[me], send_sem=send1, recv_sem=recv1,
            device_id=(peer(s), tem), device_id_type=MESH,
        ).start()
        return carry

    lax.fori_loop(1, NDEV, push, 0)
    inbox[me] = payload[me]
    choose = (
        lax.broadcasted_iota(jnp.int32, (512, 1536), 0) == target[...]
    ).astype(F32).astype(BF16)
    others = inbox.at[pl.ds(0, NDEV - 1)]
    pltpu.make_async_copy(others, others, recv1).wait()
    values = inbox[...].astype(F32).reshape(1536, 128).astype(BF16)
    sums = jnp.dot(choose, values, preferred_element_type=F32)
    weight = pltpu.roll(sums, 64, 1)
    ratio = sums / jnp.sqrt(jnp.maximum(weight, 1.0))
    low = lax.broadcasted_iota(jnp.int32, (256, 128), 1) < 64
    both = jnp.where(low, ratio[0:256], pltpu.roll(ratio[256:512], 64, 1))
    result[...] = both.reshape(NDEV, 4, 128)

    def give(s, carry):
        pltpu.make_async_remote_copy(
            src_ref=result.at[peer(s)], dst_ref=final.at[me], send_sem=send2, recv_sem=recv2,
            device_id=(peer(s), tem), device_id_type=MESH,
        ).start()
        return carry

    lax.fori_loop(1, NDEV, give, 0)
    final[me] = result[me]
    rest = final.at[pl.ds(0, NDEV - 1)]
    pltpu.make_async_copy(rest, rest, recv2).wait()
    whole = final[...]
    low = lax.broadcasted_iota(jnp.int32, (32, 128), 1) < 64
    for m in range(4):
        left, right = whole[0:32, m, :], whole[32:64, m, :]
        even = jnp.where(low, left, pltpu.roll(right, 64, 1))
        odd = jnp.where(low, pltpu.roll(left, 64, 1), right)
        out[:, m * 256 : m * 256 + 128] = even
        out[:, m * 256 + 128 : m * 256 + 256] = odd
    pltpu.make_async_copy(others, others, send1).wait()
    pltpu.make_async_copy(rest, rest, send2).wait()


def give_back(target, payload):
    vmem = pl.BlockSpec(memory_space=pltpu.VMEM)
    dma = pltpu.SemaphoreType.DMA
    return pl.pallas_call(
        return_kernel,
        out_shape=jax.ShapeDtypeStruct((32, 1024), F32),
        in_specs=[vmem, vmem],
        out_specs=vmem,
        scratch_shapes=[
            pltpu.VMEM((NDEV, 3, 8, 128), BF16),
            pltpu.VMEM((NDEV, 4, 128), F32),
            pltpu.VMEM((NDEV, 4, 128), F32),
            dma, dma, dma, dma,
        ],
        compiler_params=pltpu.CompilerParams(collective_id=2, has_side_effects=True),
    )(target, payload)


def body(across, vertical, template, science, variance, bad_pixels, patch, block):
    patch = patch.reshape(24)
    block = block.reshape(24)
    target = (block % 2) * 256 + patch * 4 + block // 2
    ids = jnp.pad(target, (0, 104)).reshape(1, 128)
    got, got_ids = gather(template.reshape(2, 16, template.shape[-1]), ids)
    payload = fit(cut_blocks(patch, block, got), science, variance, bad_pixels, across, vertical)
    targets = got_ids[:, 0, :24].reshape(1, 1536)
    return give_back(targets, payload)[None]


def solution(mesh):
    with jax.ensure_compile_time_eval():
        across, vertical = tables()
    across = jnp.asarray(across).astype(BF16)
    vertical = jnp.asarray(vertical).astype(BF16)
    return jax.shard_map(
        functools.partial(body, across, vertical),
        mesh=mesh,
        in_specs=(
            P("visit", "template", None),
            P("visit", None, "template", None),
            P("visit", None, "template", None),
            P("visit", None, "template", None),
            P("visit", None),
            P("visit", None),
        ),
        out_specs=P("visit", "template", None),
        check_vma=False,
    )
```

time: 549 us -> 131 us (0.24)
  blocking collectives: 312 us -> 0 us
  Pallas kernels: 0 us -> 124 us
  local copies, waits for them, and re-layouts: 75.3 us -> 5.32 us
  waiting for transfers between devices: 52.6 us -> 0 us
  other arithmetic: 39.7 us -> 0.01 us
  matrix products: 36.9 us -> 0 us
  starting transfers between devices: 14.4 us -> 0 us
  between operations: 13.9 us -> 0.04 us
    all_gather x2 -> x0, blocking collectives: 288 us -> none  [the longest x1 182 us: body(): lax.all_gather(intersection_block, 'visit', axis=0, tiled=True)]
    pallas_call x0 -> x4, Pallas kernels: none -> 124 us  [the longest x1 55.6 us: gather(): pl.pallas_call(gather_kernel, out_shape=(jax.ShapeDtypeStruct((2, NDEV, 1...]
    all_gather x1 -> x0, waiting for transfers between devices: 49.5 us -> none  [body(): strips = lax.all_gather(rimmed_strip[None], 'visit', axis=0, tiled=True)]
    dot_general x35 -> x0, matrix products: 36.9 us -> none  [the longest x6 14.3 us: convolve(): jnp.einsum('jbrac,jrc->ba', basis_images, usable_mask, preferred_element_...]
    all_gather x3 -> x0, local copies, waits for them, and re-layouts: 30 us -> none  [the longest x1 29.8 us: body(): strips = lax.all_gather(rimmed_strip[None], 'visit', axis=0, tiled=True)]
    psum x1 -> x0, blocking collectives: 24.5 us -> none  [body(): normal = lax.psum(partial_sums, 'template')]
    all_to_all x1 -> x0, starting transfers between devices: 11.4 us -> none  [body(): lax.all_to_all(outgoing, 'visit', split_axis=0, concat_axis=0, tiled=True)]
    broadcast_in_dim x32 -> x0, other arithmetic: 10.2 us -> none  [the longest x6 8.46 us: convolve(): jnp.concatenate([with_ones, usable_total[None], signal_total[None]])[None]]
  transfers between devices with their start and end apart: 4 -> 0, of which waited for: 2 -> 0; matrix products, arithmetic and copies ran while one was open for 1% -> 0% of each run, Pallas kernels for 0% -> 0%
where the time goes in v1:
time: 131 us; the launch traced here: 129 us
  Pallas kernels  124 us (95%)
  local copies, waits for them, and re-layouts  5.32 us (4%)
    pallas_call x1, Pallas kernels, gather(): pl.pallas_call(gather_kernel, out_shape=(jax.ShapeDtypeStruct((2, NDEV, 1...  55.6 us
    pallas_call x1, Pallas kernels, give_back(): pl.pallas_call(return_kernel, out_shape=jax.ShapeDtypeStruct((32, 1024),...  41.8 us
    pallas_call x1, Pallas kernels, fit(): pl.pallas_call(fit_kernel, out_shape=jax.ShapeDtypeStruct((NDEV, 3, 8, 12...  24 us
    unnamed x7, local copies, waits for them, and re-layouts  3.11 us

profile of v1, /device:TPU:24, one launch (start us, length us, event | category | flops | bytes accessed | tf_op | source)
XLA Modules:
  0.0 129.3 jit_solution(7350492199316364423)
XLA Ops:
  0.0 0.8 copy.12
  0.8 0.1 reshape.14.patch
  0.8 0.0 copy-start
  0.9 0.8 copy.11
  1.6 0.1 reshape.13.block
  1.7 0.0 copy-start.1
  1.7 0.5 pad_bitcast_fusion.ids
  2.2 55.6 %shard_map.82 = (bf16[2,64,16,1152]{3,2,1,0:T(8,128)(2,1)}, s32[64,1,128]{2,1,0:T(1,128)}) custom-call(bf16[2,16,1152]{2,1,0:T(8,128)(2,1)} %bitcast.5, s32[1,128]{1,0:T(1,128)} %pad_bitcast_fusion.ids), custom_call_target="tpu_custom_call" | custom-call | tf_op jit(solution)/shard_map/pallas_call | solution.py:168
  57.9 0.8 slice_reduce_fusion
  58.7 0.7 reshape_squeeze.3.target
  59.4 0.0 copy-done
  59.4 0.0 copy-done.1
  59.4 2.5 %shard_map.83.core = bf16[2,24,16,256]{3,2,1,0:T(8,128)(2,1)} custom-call(s32[24]{0:T(128)} %copy-done, s32[24]{0:T(128)} %copy-done.1, bf16[2,64,16,1152]{3,2,1,0:T(8,128)(2,1)} %get-tuple-element.8.got), custom_call_target="tpu_custom_call" | custom-call | tf_op jit(solution)/shard_map/pallas_call | solution.py:195
  61.9 24.0 %shard_map.84.payload = bf16[64,3,8,128]{3,2,1,0:T(8,128)(2,1)} custom-call(bf16[2,24,16,256]{3,2,1,0:T(8,128)(2,1)} %shard_map.83.core, bf16[6,4,32,128]{3,2,1,0:T(8,128)(2,1)} %science.1, bf16[6,4,32,128]{3,2,1,0:T(8,128)(2,1)} %variance.1, s32[6,4,32,128]{3,2,1,0:T(8,128)} %bad.1, bf16[256,512]{1,0:T(8,128)(2,1)} %constant.35.clone.across, ...), custom_call_target="tpu_custom_call" | custom-call | tf_op jit(solution)/shard_map/pallas_call | solution.py:373
  85.9 41.8 %shard_map.85 = f32[32,1024]{1,0:T(8,128)} custom-call(s32[1,1536]{1,0:T(1,128)} %reshape_squeeze.3.target, bf16[64,3,8,128]{3,2,1,0:T(8,128)(2,1)} %shard_map.84.payload), custom_call_target="tpu_custom_call" | custom-call | tf_op jit(solution)/shard_map/pallas_call | solution.py:457
  127.7 1.6 %copy.14 = f32[1,32,1024]{2,1,0:T(8,128)} copy(f32[1,32,1024]{2,1,0:T(8,128)} %bitcast.4) | data formatting | bytes 262144
  (1 shorter events, 0.0 us)
Async XLA Ops:
  0.8 58.5 %copy-start = (s32[24]{0:T(128)}, s32[24]{0:T(128)S(1)}, u32[]{:S(2)}) copy-start(s32[24]{0:T(128)S(1)} %reshape.14.patch) | copy-start | bytes 292
  1.7 57.7 %copy-start.1 = (s32[24]{0:T(128)}, s32[24]{0:T(128)S(1)}, u32[]{:S(2)}) copy-start(s32[24]{0:T(128)S(1)} %reshape.13.block) | copy-start | bytes 292

commit v2 on v1

v2 whole, which is shorter than its diff:
```python
import functools

import jax
import jax.numpy as jnp
import numpy as np
from jax import lax
from jax.experimental import pallas as pl
from jax.experimental.pallas import tpu as pltpu
from jax.sharding import PartitionSpec as P

NBLK = 8
MARGIN = 64
HALF = 10
RIDGE = 0.05
NZ, NY = 16, 4
NDEV = NZ * NY
NTEM = 8
MESH = pl.DeviceIdType.MESH
F32 = jnp.float32
BF16 = jnp.bfloat16


def basis_taps():
    spread = jnp.arange(2 * HALF + 1, dtype=jnp.float32)
    scaled = (HALF - spread) / 2.5
    hermite = jnp.stack(
        [
            jnp.ones(scaled.shape, jnp.float32),
            2.0 * scaled,
            4.0 * scaled * scaled - 2.0,
            8.0 * scaled * scaled * scaled - 12.0 * scaled,
        ]
    )
    shaped = hermite * jnp.exp(-0.5 * scaled * scaled)
    shaped = shaped / jnp.sqrt(jnp.sum(shaped * shaped, axis=1, keepdims=True))
    return shaped.astype(jnp.bfloat16)


def tables():
    profile = np.asarray(basis_taps().astype(jnp.float32))
    across = np.zeros((256, 4, 128), np.float32)
    vertical = np.zeros((4, 32, 64), np.float32)
    for t in range(2 * HALF + 1):
        for c in range(128):
            across[c + t + MARGIN - HALF, :, c] = profile[:, t]
        for r in range(32):
            vertical[:, r, r + t + 16 - HALF] = profile[:, t]
    return across.reshape(256, 512), vertical.reshape(128, 64)


def wrap(value, size):
    return lax.rem(value + size, size)


TILES = 9
LEAD = 7
SLOTS = 24
HALFWAY = (1, -1)
Y_STEP = {0: 0, 1: 1, 2: 2, 3: -1}


def kernel(
    patch, block, strip, science, variance, bad, across, vertical, out,
    stage, got, packed, early, late, early_in, late_in, core, rim, smooth, images,
    part, parts, rows, coef, choose, spread, result, final,
    local_sem, send_sem, ay, az, bz, by, halo_send, halo_recv, sum_send, sum_recv,
    early_send, early_recv, late_send, late_recv, final_send, final_recv,
):
    me = lax.axis_index("visit")
    tem = lax.axis_index("template")
    z, y = lax.div(me, NY), lax.rem(me, NY)
    visits = science.shape[0]

    def at(dz, dy):
        return (wrap(z + dz, NZ) * NY + wrap(y + dy, NY), tem)

    def beside(step):
        return (me, wrap(tem + step, NTEM))

    def send(src, dst, sem, recv, target):
        copy = pltpu.make_async_remote_copy(
            src_ref=src, dst_ref=dst, send_sem=sem, recv_sem=recv,
            device_id=target, device_id_type=MESH,
        )
        copy.start()
        return copy

    def arrive(ref, sem):
        pltpu.make_async_copy(ref, ref, sem).wait()

    barrier = pltpu.get_barrier_semaphore()
    partners = [at(0, 1), at(0, -1), at(0, 2), at(1, 0), at(-1, 0)]
    partners += [beside(d) for d in range(1, NTEM)]
    for partner in partners:
        pl.semaphore_signal(barrier, inc=1, device_id=partner, device_id_type=MESH)

    for h in range(2):
        for c in range(TILES):
            pltpu.make_async_copy(
                strip.at[pl.ds(16 * h, 16), pl.ds(128 * c, 128)],
                stage.at[h * TILES + c],
                local_sem,
            ).start()

    low = lax.broadcasted_iota(jnp.int32, (32, 128), 1) < 64
    for v in range(visits):
        for j in range(4):
            weight = (1 - bad[v, j]).astype(F32) / variance[v, j].astype(F32)
            code = (block[v, j] & 1) * 256 + patch[v, j] * 4 + (block[v, j] >> 1) - 256
            code = jnp.full((32, 128), code, jnp.int32).astype(F32)
            packed[pl.ds(v * 4 + j, 32, stride=SLOTS), :] = jnp.where(
                low, code, pltpu.roll(weight, 64, 1)
            )
            packed[pl.ds(768 + v * 4 + j, 32, stride=SLOTS), :] = jnp.where(low, code, weight)
    early[...] = packed[...].reshape(NDEV, 3, 8, 128).astype(BF16)

    arrive(stage, local_sem)
    pl.semaphore_wait(barrier, len(partners))

    def slot(zz, yy):
        return wrap(zz, NZ) * NY + wrap(yy, NY)

    def a_ref(zz, yy):
        return got.at[slot(zz, yy), pl.ds(0, LEAD)]

    def b_ref(zz, yy):
        return got.at[slot(zz, yy), pl.ds(LEAD, 2 * TILES - LEAD)]

    a_own, b_own = stage.at[pl.ds(0, LEAD)], stage.at[pl.ds(LEAD, 2 * TILES - LEAD)]
    for d in (1, 3, 2):
        send(a_own, a_ref(z, y), send_sem, ay.at[d - 1], at(0, Y_STEP[d]))
    for k, dz in enumerate(HALFWAY):
        send(b_own, b_ref(z, y), send_sem, bz.at[k, 0], at(dz, 0))
        send(a_own, a_ref(z, y), send_sem, az.at[k, 0, 0], at(dz, 0))
    for k, dy in enumerate(HALFWAY):
        send(b_own, b_ref(z, y), send_sem, by.at[k, 0], at(0, dy))
    got[me] = stage[...]
    for d in (1, 3, 2):
        ref = a_ref(z, y - Y_STEP[d])
        arrive(ref, ay.at[d - 1])
        for k, dz in enumerate(HALFWAY):
            send(ref, ref, send_sem, az.at[k, 0, d], at(dz, 0))

    def relay(source, index):
        k = index % 2
        dy = HALFWAY[k]
        ref = b_ref(source, y - dy)
        arrive(ref, by.at[k, index])
        send(ref, ref, send_sem, by.at[2, index], at(0, dy))

    ring = NZ // 2
    for s in range(1, ring + 1):
        for k, dz in enumerate(HALFWAY):
            if s == ring and k == 1:
                continue
            ref = b_ref(z - dz * s, y)
            arrive(ref, bz.at[k, s - 1])
            if s < ring - k:
                send(ref, ref, send_sem, bz.at[k, s], at(dz, 0))
            for q, dy in enumerate(HALFWAY):
                send(ref, ref, send_sem, by.at[q, 2 * s - 1 + k], at(0, dy))
        for d in (0, 1, 3, 2):
            for k, dz in enumerate(HALFWAY):
                if s == ring and k != (d >= 2):
                    continue
                ref = a_ref(z - dz * s, y - Y_STEP[d])
                arrive(ref, az.at[k, s - 1, d])
                if s < ring - 1 or (s == ring - 1 and k == (d >= 2)):
                    send(ref, ref, send_sem, az.at[k, s, d], at(dz, 0))
        if s == 1:
            relay(z, 0)
        else:
            for k, dz in enumerate(HALFWAY):
                relay(z - dz * (s - 1), 2 * (s - 1) - 1 + k)
    relay(z - ring, NZ - 1)
    for index in range(NZ):
        s = (index + 1) // 2
        source = z - s if index % 2 == 1 else z + s
        k = index % 2
        arrive(b_ref(source, y + HALFWAY[k]), by.at[1 - k, index])
        arrive(b_ref(source, y + 2), by.at[2, index])

    def peer(s):
        return lax.rem(me + s, NDEV)

    def push(source, dest, sem, recv):
        def one(s, carry):
            send(source.at[peer(s)], dest.at[me], sem, recv, (peer(s), tem))
            return carry

        lax.fori_loop(1, NDEV, one, 0)

    push(early, early_in, early_send, early_recv)

    for v in range(visits):
        for j in range(4):
            p, b = patch[v, j], block[v, j]
            for h in range(2):
                core[h, v * 4 + j, :, 0:128] = got[p, h * TILES + b]
                core[h, v * 4 + j, :, 128:256] = got[p, h * TILES + b + 1]

    def halo(source, dest, step, k):
        return pltpu.make_async_remote_copy(
            src_ref=core.at[source], dst_ref=rim.at[dest],
            send_sem=halo_send.at[k], recv_sem=halo_recv.at[k],
            device_id=beside(step), device_id_type=MESH,
        )

    down, up = halo(1, 0, 1, 0), halo(0, 1, -1, 1)

    @pl.when(tem < NTEM - 1)
    def _():
        down.start()

    @pl.when(tem > 0)
    def _():
        up.start()

    def smear(piece, source):
        image = jnp.dot(
            source.reshape(SLOTS * 16, 256), across[...], preferred_element_type=F32
        )
        smooth[:, piece * 16 : piece * 16 + 16, :] = image.astype(BF16).reshape(SLOTS, 16, 512)

    early_in[me] = early[me]
    smear(1, core[0])
    smear(2, core[1])

    @pl.when(tem == 0)
    def _():
        rim[0] = jnp.zeros((SLOTS, 16, 256), BF16)

    @pl.when(tem == NTEM - 1)
    def _():
        rim[1] = jnp.zeros((SLOTS, 16, 256), BF16)

    @pl.when(tem > 0)
    def _():
        down.wait_recv()

    smear(0, rim[0])

    @pl.when(tem < NTEM - 1)
    def _():
        up.wait_recv()

    smear(3, rim[1])
    part[...] = jnp.zeros((24, 128), F32)
    row_id = lax.broadcasted_iota(jnp.int32, (544, 576), 0) & 31
    lane_id = lax.broadcasted_iota(jnp.int32, (544, 576), 1) & 31
    same_row = row_id == lane_id
    pick_row = lax.broadcasted_iota(jnp.int32, (576, 128), 0) >> 5
    pick_lane = lax.broadcasted_iota(jnp.int32, (576, 128), 1)

    def gram(v, carry):
        for j in range(4):
            image = jnp.dot(
                vertical[...], smooth[v * 4 + j], preferred_element_type=F32
            ).astype(BF16)
            for a in range(4):
                images[v, a * 128 : a * 128 + 128, j * 128 : j * 128 + 128] = image[
                    :, a * 128 : a * 128 + 128
                ]
        usable = jnp.concatenate(
            [(1 - bad[v, j]).astype(F32).astype(BF16) for j in range(4)], axis=1
        )
        signal = jnp.concatenate([science[v, j] for j in range(4)], axis=1)
        left = images[v]
        right = jnp.concatenate(
            [left * jnp.concatenate([usable] * 16, axis=0), usable, usable * signal], axis=0
        )
        left = jnp.concatenate([left, usable], axis=0)
        full = lax.dot_general(
            left, right, (((1,), (1,)), ((), ())), preferred_element_type=F32
        )
        full = jnp.where(same_row, full, 0.0)
        sums = jnp.sum(full.reshape(17, 32, 576), axis=1)
        pick = (pick_lane == pick_row + v * 20).astype(F32)
        part[0:17, :] += jnp.dot(
            sums, pick, preferred_element_type=F32, precision=lax.Precision.HIGHEST
        )
        return carry

    lax.fori_loop(0, visits, gram, 0)

    for d in range(1, NTEM):
        send(part, parts.at[tem], sum_send, sum_recv, beside(d))
    parts[tem] = part[...]
    seven = parts.at[pl.ds(0, NTEM - 1)]
    arrive(seven, sum_recv)
    total = parts[0]
    for d in range(1, NTEM):
        total = total + parts[d]

    rows[...] = jnp.zeros((192, 128), F32)
    for v in range(visits):
        moved = total if v == 0 else pltpu.roll(total, 128 - 20 * v, 1)
        rows[pl.ds(v, 24, stride=8), :] = moved
    lane = lax.broadcasted_iota(jnp.int32, (8, 128), 1)
    system = [rows[k * 8 : k * 8 + 8, :] for k in range(17)]
    ridge = RIDGE * (system[16][:, 16:17] + 1.0)
    system = [jnp.where(lane == k, system[k] + ridge, system[k]) for k in range(17)]
    for c in range(17):
        pivot = system[c] / system[c][:, c : c + 1]
        system = [
            pivot if k == c else system[k] - system[k][:, c : c + 1] * pivot for k in range(17)
        ]
    for k in range(17):
        coef[k] = jnp.broadcast_to(system[k][:, 17:18], (8, 128))

    def differ(v, carry):
        for j in range(4):
            numbers = []
            for w in (v, v + 3):
                model = jnp.broadcast_to(coef[16, pl.ds(w, 1), :], (32, 128))
                for k in range(16):
                    factor = jnp.broadcast_to(coef[k, pl.ds(w, 1), :], (32, 128))
                    image = images[w, k * 32 : k * 32 + 32, j * 128 : j * 128 + 128]
                    model = model + factor * image.astype(F32)
                weight = (1 - bad[w, j]).astype(F32) / variance[w, j].astype(F32)
                numbers.append(weight * (science[w, j].astype(F32) - model))
            here, there = numbers
            packed[pl.ds(v * 4 + j, 32, stride=12), :] = jnp.where(
                low, here, pltpu.roll(there, 64, 1)
            )
            packed[pl.ds(384 + v * 4 + j, 32, stride=12), :] = jnp.where(
                low, pltpu.roll(here, 64, 1), there
            )
        return carry

    lax.fori_loop(0, visits // 2, differ, 0)
    for k in range(NDEV):
        late[k] = packed[k * 12 : k * 12 + 12, :].astype(BF16)
    push(late, late_in, late_send, late_recv)
    late_in[me] = late[me]

    arrive(early_in.at[pl.ds(0, NDEV - 1)], early_recv)
    values = early_in[...].astype(F32).reshape(NDEV * SLOTS, 128)
    lanes = lax.broadcasted_iota(jnp.int32, (NDEV * SLOTS, 128), 1)
    code = jnp.where(lanes < 64, values, pltpu.roll(values, 64, 1))
    place = lanes.astype(F32)
    for q in range(4):
        choose[:, q * 128 : q * 128 + 128] = jnp.where(
            code == place + (q * 128.0 - 256.0), 1.0, 0.0
        ).astype(BF16)
    inner = (((0,), (0,)), ((), ()))
    denominator = lax.dot_general(
        values.astype(BF16), choose[...], inner, preferred_element_type=F32
    )[64:128]
    scale = jnp.sqrt(jnp.maximum(denominator, 1.0))

    arrive(late_in.at[pl.ds(0, NDEV - 1)], late_recv)
    for k in range(NDEV):
        value = late_in[k].astype(F32)
        spread[k, 0:12, :] = value
        spread[k, 12:24, :] = pltpu.roll(value, 64, 1)
    numerator = lax.dot_general(
        spread[...].reshape(NDEV * SLOTS, 128).astype(BF16), choose[...], inner,
        preferred_element_type=F32,
    )[0:64]
    ratio = numerator / scale
    both = jnp.concatenate([ratio[:, 0:256], ratio[:, 256:512]], axis=0).T
    result[...] = both.reshape(NDEV, 4, 128)
    push(result, final, final_send, final_recv)
    final[me] = result[me]
    arrive(final.at[pl.ds(0, NDEV - 1)], final_recv)
    whole = final[...]
    for m in range(4):
        left, right = whole[0:32, m, :], whole[32:64, m, :]
        out[:, m * 256 : m * 256 + 128] = jnp.where(low, left, pltpu.roll(right, 64, 1))
        out[:, m * 256 + 128 : m * 256 + 256] = jnp.where(low, pltpu.roll(left, 64, 1), right)

    arrive(got.at[pl.ds(0, NDEV - 1)], send_sem)
    arrive(seven, sum_send)
    arrive(early.at[pl.ds(0, NDEV - 1)], early_send)
    arrive(late.at[pl.ds(0, NDEV - 1)], late_send)
    arrive(result.at[pl.ds(0, NDEV - 1)], final_send)

    @pl.when(tem < NTEM - 1)
    def _():
        down.wait_send()

    @pl.when(tem > 0)
    def _():
        up.wait_send()


def body(across, vertical, template, science, variance, bad_pixels, patch, block):
    vmem = pl.BlockSpec(memory_space=pltpu.VMEM)
    smem = pl.BlockSpec(memory_space=pltpu.SMEM)
    anywhere = pl.BlockSpec(memory_space=pl.ANY)
    dma = pltpu.SemaphoreType.DMA
    return pl.pallas_call(
        kernel,
        out_shape=jax.ShapeDtypeStruct((32, 1024), F32),
        in_specs=[smem, smem, anywhere] + [vmem] * 5,
        out_specs=vmem,
        scratch_shapes=[
            pltpu.VMEM((18, 16, 128), BF16),
            pltpu.VMEM((NDEV, 18, 16, 128), BF16),
            pltpu.VMEM((1536, 128), F32),
            pltpu.VMEM((NDEV, 3, 8, 128), BF16),
            pltpu.VMEM((NDEV, 12, 128), BF16),
            pltpu.VMEM((NDEV, 3, 8, 128), BF16),
            pltpu.VMEM((NDEV, 12, 128), BF16),
            pltpu.VMEM((2, SLOTS, 16, 256), BF16),
            pltpu.VMEM((2, SLOTS, 16, 256), BF16),
            pltpu.VMEM((SLOTS, 64, 512), BF16),
            pltpu.VMEM((6, 512, 512), BF16),
            pltpu.VMEM((24, 128), F32),
            pltpu.VMEM((NTEM, 24, 128), F32),
            pltpu.VMEM((192, 128), F32),
            pltpu.VMEM((17, 8, 128), F32),
            pltpu.VMEM((1536, 512), BF16),
            pltpu.VMEM((NDEV, SLOTS, 128), F32),
            pltpu.VMEM((NDEV, 4, 128), F32),
            pltpu.VMEM((NDEV, 4, 128), F32),
            dma, dma, dma((3,)), dma((2, 8, 4)), dma((2, 8)), dma((3, NZ)),
            dma((2,)), dma((2,)), dma, dma, dma, dma, dma, dma, dma, dma,
        ],
        compiler_params=pltpu.CompilerParams(collective_id=0, has_side_effects=True),
    )(patch, block, template[0], science, variance, bad_pixels, across, vertical)[None]


def solution(mesh):
    with jax.ensure_compile_time_eval():
        across, vertical = tables()
    across = jnp.asarray(across).astype(BF16)
    vertical = jnp.asarray(vertical).astype(BF16)
    return jax.shard_map(
        functools.partial(body, across, vertical),
        mesh=mesh,
        in_specs=(
            P("visit", "template", None),
            P("visit", None, "template", None),
            P("visit", None, "template", None),
            P("visit", None, "template", None),
            P("visit", None),
            P("visit", None),
        ),
        out_specs=P("visit", "template", None),
        check_vma=False,
    )
```

time: 131 us -> 103 us (0.79)
  Pallas kernels: 124 us -> 98.5 us
  local copies, waits for them, and re-layouts: 5.32 us -> 3.62 us
    pallas_call x4 -> x1, Pallas kernels: 124 us -> 98.5 us  [body(): pl.pallas_call(kernel, out_shape=jax.ShapeDtypeStruct((32, 1024), F32), i...]
    unnamed x7 -> x5, local copies, waits for them, and re-layouts: 3.11 us -> 3.62 us
where the time goes in v2:
time: 103 us; the launch traced here: 102 us
  Pallas kernels  98.5 us (96%)
  local copies, waits for them, and re-layouts  3.62 us (4%)
    pallas_call x1, Pallas kernels, body(): pl.pallas_call(kernel, out_shape=jax.ShapeDtypeStruct((32, 1024), F32), i...  98.5 us
    unnamed x5, local copies, waits for them, and re-layouts  3.62 us

profile of v2, /device:TPU:24, one launch (start us, length us, event | category | flops | bytes accessed | tf_op | source)
XLA Modules:
  0.0 102.2 jit_solution(10575108108660605430)
XLA Ops:
  0.0 0.0 copy-start
  0.0 1.4 %copy.9.patch = s32[6,4]{1,0:T(8,128)} copy(s32[6,4]{0,1:T(4,128)} %param.12) | data formatting | bytes 192 | tf_op args[4]
  1.4 0.0 copy-done
  1.4 0.7 copy.10.block
  2.1 98.5 %shard_map.82 = f32[32,1024]{1,0:T(8,128)} custom-call(s32[6,4]{1,0:T(8,128)} %copy.9.patch, s32[6,4]{1,0:T(8,128)} %copy.10.block, bf16[32,1152]{1,0:T(8,128)(2,1)} %bitcast.3, bf16[6,4,32,128]{3,2,1,0:T(8,128)(2,1)} %science.1, bf16[6,4,32,128]{3,2,1,0:T(8,128)(2,1)} %variance.1, s32[6,4,32,128]{3,2,1,0:T(8,128)} %bad.1, ...), custom_call_target="tpu_custom_call" | custom-call | tf_op jit(solution)/shard_map/pallas_call | solution.py:393
  100.6 1.6 %copy.12 = f32[1,32,1024]{2,1,0:T(8,128)} copy(f32[1,32,1024]{2,1,0:T(8,128)} %bitcast.2) | data formatting | bytes 262144
Async XLA Ops:
  0.0 1.4 %copy-start = (s32[6,4]{0,1:T(4,128)S(1)}, s32[6,4]{0,1:T(4,128)}, u32[]{:S(2)}) copy-start(s32[6,4]{0,1:T(4,128)} %param.13) | copy-start | bytes 292

commit v3 on v2

--- a/solution.py
+++ b/solution.py
@@ -53,7 +53,7 @@
 
 
 TILES = 9
-LEAD = 7
+LEAD = 8
 SLOTS = 24
 HALFWAY = (1, -1)
 Y_STEP = {0: 0, 1: 1, 2: 2, 3: -1}
@@ -62,7 +62,7 @@
 def kernel(
     patch, block, strip, science, variance, bad, across, vertical, out,
     stage, got, packed, early, late, early_in, late_in, core, rim, smooth, images,
-    part, parts, rows, coef, choose, spread, result, final,
+    sums, part, parts, rows, coef, codes, column, choose, spread, result, final,
     local_sem, send_sem, ay, az, bz, by, halo_send, halo_recv, sum_send, sum_recv,
     early_send, early_recv, late_send, late_recv, final_send, final_recv,
 ):
@@ -103,16 +103,27 @@
             ).start()
 
     low = lax.broadcasted_iota(jnp.int32, (32, 128), 1) < 64
+    lane = lax.broadcasted_iota(jnp.int32, (8, 128), 1)
+
+    def weigh(v, j):
+        return (1 - bad[v, j]).astype(F32) / variance[v, j].astype(F32)
+
+    def pack(index, here, there, pitch):
+        packed[pl.ds(index, 32, stride=pitch), :] = jnp.where(low, here, pltpu.roll(there, 64, 1))
+        packed[pl.ds(32 * pitch + index, 32, stride=pitch), :] = jnp.where(
+            low, pltpu.roll(here, 64, 1), there
+        )
+
+    targets = jnp.zeros((8, 128), F32)
     for v in range(visits):
         for j in range(4):
-            weight = (1 - bad[v, j]).astype(F32) / variance[v, j].astype(F32)
-            code = (block[v, j] & 1) * 256 + patch[v, j] * 4 + (block[v, j] >> 1) - 256
-            code = jnp.full((32, 128), code, jnp.int32).astype(F32)
-            packed[pl.ds(v * 4 + j, 32, stride=SLOTS), :] = jnp.where(
-                low, code, pltpu.roll(weight, 64, 1)
-            )
-            packed[pl.ds(768 + v * 4 + j, 32, stride=SLOTS), :] = jnp.where(low, code, weight)
-    early[...] = packed[...].reshape(NDEV, 3, 8, 128).astype(BF16)
+            code = (block[j, v] & 1) * 256 + patch[j, v] * 4 + (block[j, v] >> 1) - 256
+            code = jnp.full((8, 128), code, jnp.int32).astype(F32)
+            targets = jnp.where(lane == v * 4 + j, code, targets)
+            if v < visits // 2:
+                pack(v * 4 + j, weigh(v, j), weigh(v + 3, j), 16)
+    packed[pl.ds(12, NDEV, stride=16), :] = jnp.broadcast_to(targets[0:1], (NDEV, 128))
+    early[...] = packed[...].reshape(NDEV, 16, 128).astype(BF16)
 
     arrive(stage, local_sem)
     pl.semaphore_wait(barrier, len(partners))
@@ -184,17 +195,20 @@
         return lax.rem(me + s, NDEV)
 
     def push(source, dest, sem, recv):
-        def one(s, carry):
+        def one(s):
             send(source.at[peer(s)], dest.at[me], sem, recv, (peer(s), tem))
+
+        def two(m, carry):
+            one(NDEV // 2 - m)
+            one(NDEV // 2 + m)
             return carry
 
-        lax.fori_loop(1, NDEV, one, 0)
-
-    push(early, early_in, early_send, early_recv)
+        one(NDEV // 2)
+        lax.fori_loop(1, NDEV // 2, two, 0)
 
     for v in range(visits):
         for j in range(4):
-            p, b = patch[v, j], block[v, j]
+            p, b = patch[j, v], block[j, v]
             for h in range(2):
                 core[h, v * 4 + j, :, 0:128] = got[p, h * TILES + b]
                 core[h, v * 4 + j, :, 128:256] = got[p, h * TILES + b + 1]
@@ -222,6 +236,7 @@
         )
         smooth[:, piece * 16 : piece * 16 + 16, :] = image.astype(BF16).reshape(SLOTS, 16, 512)
 
+    push(early, early_in, early_send, early_recv)
     early_in[me] = early[me]
     smear(1, core[0])
     smear(2, core[1])
@@ -245,44 +260,54 @@
         up.wait_recv()
 
     smear(3, rim[1])
-    part[...] = jnp.zeros((24, 128), F32)
-    row_id = lax.broadcasted_iota(jnp.int32, (544, 576), 0) & 31
-    lane_id = lax.broadcasted_iota(jnp.int32, (544, 576), 1) & 31
+    row_id = lax.broadcasted_iota(jnp.int32, (144, 144), 0) & 7
+    lane_id = lax.broadcasted_iota(jnp.int32, (144, 144), 1) & 7
     same_row = row_id == lane_id
-    pick_row = lax.broadcasted_iota(jnp.int32, (576, 128), 0) >> 5
-    pick_lane = lax.broadcasted_iota(jnp.int32, (576, 128), 1)
 
     def gram(v, carry):
+        ones, extra = [None] * 16, [None] * 16
         for j in range(4):
-            image = jnp.dot(
-                vertical[...], smooth[v * 4 + j], preferred_element_type=F32
-            ).astype(BF16)
-            for a in range(4):
-                images[v, a * 128 : a * 128 + 128, j * 128 : j * 128 + 128] = image[
-                    :, a * 128 : a * 128 + 128
-                ]
-        usable = jnp.concatenate(
-            [(1 - bad[v, j]).astype(F32).astype(BF16) for j in range(4)], axis=1
-        )
-        signal = jnp.concatenate([science[v, j] for j in range(4)], axis=1)
+            image = jnp.dot(vertical[...], smooth[v * 4 + j], preferred_element_type=F32)
+            usable = (1 - bad[v, j]).astype(F32)
+            masked = usable * science[v, j].astype(F32)
+            for g in range(4):
+                tile = g * 4 + j
+                rows_of = slice(g * 8, g * 8 + 8)
+                for a in range(4):
+                    pieces = [
+                        image[b * 32 + g * 8 : b * 32 + g * 8 + 8, a * 128 : a * 128 + 128]
+                        for b in range(4)
+                    ]
+                    images[v, a * 32 : a * 32 + 32, tile * 128 : tile * 128 + 128] = (
+                        jnp.concatenate(pieces, axis=0).astype(BF16)
+                    )
+                some = usable[rows_of]
+                ones[tile] = jnp.concatenate([some, some], axis=0).astype(BF16)
+                extra[tile] = jnp.concatenate([some, masked[rows_of]], axis=0).astype(BF16)
+        ones = jnp.concatenate(ones, axis=1)
+        extra = jnp.concatenate(extra, axis=1)
         left = images[v]
-        right = jnp.concatenate(
-            [left * jnp.concatenate([usable] * 16, axis=0), usable, usable * signal], axis=0
-        )
-        left = jnp.concatenate([left, usable], axis=0)
+        right = jnp.concatenate([left * jnp.concatenate([ones] * 8, axis=0), extra], axis=0)
+        left = jnp.concatenate([left, extra], axis=0)
         full = lax.dot_general(
             left, right, (((1,), (1,)), ((), ())), preferred_element_type=F32
         )
         full = jnp.where(same_row, full, 0.0)
-        sums = jnp.sum(full.reshape(17, 32, 576), axis=1)
-        pick = (pick_lane == pick_row + v * 20).astype(F32)
-        part[0:17, :] += jnp.dot(
-            sums, pick, preferred_element_type=F32, precision=lax.Precision.HIGHEST
-        )
+        sums[v, 0:18, :] = jnp.sum(full.reshape(18, 8, 144), axis=1)
+        sums[v, 18:24, :] = jnp.zeros((6, 144), F32)
         return carry
 
     lax.fori_loop(0, visits, gram, 0)
-
+    pick_row = lax.broadcasted_iota(jnp.int32, (144, 128), 0) >> 3
+    pick_lane = lax.broadcasted_iota(jnp.int32, (144, 128), 1)
+    dense = jnp.dot(
+        sums[...].reshape(144, 144), (pick_lane == pick_row).astype(F32),
+        preferred_element_type=F32, precision=lax.Precision.HIGHEST,
+    )
+    mine = dense[0:24]
+    for v in range(1, visits):
+        mine = mine + pltpu.roll(dense[v * 24 : v * 24 + 24], 20 * v, 1)
+    part[...] = mine
     for d in range(1, NTEM):
         send(part, parts.at[tem], sum_send, sum_recv, beside(d))
     parts[tem] = part[...]
@@ -296,7 +321,6 @@
     for v in range(visits):
         moved = total if v == 0 else pltpu.roll(total, 128 - 20 * v, 1)
         rows[pl.ds(v, 24, stride=8), :] = moved
-    lane = lax.broadcasted_iota(jnp.int32, (8, 128), 1)
     system = [rows[k * 8 : k * 8 + 8, :] for k in range(17)]
     ridge = RIDGE * (system[16][:, 16:17] + 1.0)
     system = [jnp.where(lane == k, system[k] + ridge, system[k]) for k in range(17)]
@@ -309,23 +333,25 @@
         coef[k] = jnp.broadcast_to(system[k][:, 17:18], (8, 128))
 
     def differ(v, carry):
+        numbers = []
+        for w in (v, v + 3):
+            factors = [jnp.broadcast_to(coef[k, pl.ds(w, 1), :], (8, 128)) for k in range(17)]
+            for j in range(4):
+                models = []
+                for g in range(4):
+                    tile = g * 4 + j
+                    model = factors[16]
+                    for a in range(4):
+                        image = images[
+                            w, a * 32 : a * 32 + 32, tile * 128 : tile * 128 + 128
+                        ].astype(F32)
+                        for b in range(4):
+                            model = model + factors[a * 4 + b] * image[b * 8 : b * 8 + 8]
+                    models.append(model)
+                model = jnp.concatenate(models, axis=0)
+                numbers.append(weigh(w, j) * (science[w, j].astype(F32) - model))
         for j in range(4):
-            numbers = []
-            for w in (v, v + 3):
-                model = jnp.broadcast_to(coef[16, pl.ds(w, 1), :], (32, 128))
-                for k in range(16):
-                    factor = jnp.broadcast_to(coef[k, pl.ds(w, 1), :], (32, 128))
-                    image = images[w, k * 32 : k * 32 + 32, j * 128 : j * 128 + 128]
-                    model = model + factor * image.astype(F32)
-                weight = (1 - bad[w, j]).astype(F32) / variance[w, j].astype(F32)
-                numbers.append(weight * (science[w, j].astype(F32) - model))
-            here, there = numbers
-            packed[pl.ds(v * 4 + j, 32, stride=12), :] = jnp.where(
-                low, here, pltpu.roll(there, 64, 1)
-            )
-            packed[pl.ds(384 + v * 4 + j, 32, stride=12), :] = jnp.where(
-                low, pltpu.roll(here, 64, 1), there
-            )
+            pack(v * 4 + j, numbers[j], numbers[4 + j], 12)
         return carry
 
     lax.fori_loop(0, visits // 2, differ, 0)
@@ -335,18 +361,26 @@
     late_in[me] = late[me]
 
     arrive(early_in.at[pl.ds(0, NDEV - 1)], early_recv)
-    values = early_in[...].astype(F32).reshape(NDEV * SLOTS, 128)
-    lanes = lax.broadcasted_iota(jnp.int32, (NDEV * SLOTS, 128), 1)
-    code = jnp.where(lanes < 64, values, pltpu.roll(values, 64, 1))
-    place = lanes.astype(F32)
+    codes[...] = jnp.zeros((128, 128), F32)
+    for k in range(NDEV):
+        value = early_in[k].astype(F32)
+        spread[k, 0:12, :] = value[0:12]
+        spread[k, 12:24, :] = pltpu.roll(value[0:12], 64, 1)
+        codes[k : k + 1, :] = value[12:13]
+    across_codes = codes[...].T
+    for k in range(NDEV):
+        column[k] = jnp.broadcast_to(across_codes[0:SLOTS, k : k + 1], (SLOTS, 128))
+    code = column[...].reshape(NDEV * SLOTS, 128)
+    place = lax.broadcasted_iota(jnp.int32, (NDEV * SLOTS, 128), 1).astype(F32)
     for q in range(4):
         choose[:, q * 128 : q * 128 + 128] = jnp.where(
             code == place + (q * 128.0 - 256.0), 1.0, 0.0
         ).astype(BF16)
     inner = (((0,), (0,)), ((), ()))
     denominator = lax.dot_general(
-        values.astype(BF16), choose[...], inner, preferred_element_type=F32
-    )[64:128]
+        spread[...].reshape(NDEV * SLOTS, 128).astype(BF16), choose[...], inner,
+        preferred_element_type=F32,
+    )[0:64]
     scale = jnp.sqrt(jnp.maximum(denominator, 1.0))
 
     arrive(late_in.at[pl.ds(0, NDEV - 1)], late_recv)
@@ -398,19 +432,22 @@
         scratch_shapes=[
             pltpu.VMEM((18, 16, 128), BF16),
             pltpu.VMEM((NDEV, 18, 16, 128), BF16),
-            pltpu.VMEM((1536, 128), F32),
-            pltpu.VMEM((NDEV, 3, 8, 128), BF16),
+            pltpu.VMEM((1024, 128), F32),
+            pltpu.VMEM((NDEV, 16, 128), BF16),
             pltpu.VMEM((NDEV, 12, 128), BF16),
-            pltpu.VMEM((NDEV, 3, 8, 128), BF16),
+            pltpu.VMEM((NDEV, 16, 128), BF16),
             pltpu.VMEM((NDEV, 12, 128), BF16),
             pltpu.VMEM((2, SLOTS, 16, 256), BF16),
             pltpu.VMEM((2, SLOTS, 16, 256), BF16),
             pltpu.VMEM((SLOTS, 64, 512), BF16),
-            pltpu.VMEM((6, 512, 512), BF16),
+            pltpu.VMEM((6, 128, 2048), BF16),
+            pltpu.VMEM((6, 24, 144), F32),
             pltpu.VMEM((24, 128), F32),
             pltpu.VMEM((NTEM, 24, 128), F32),
             pltpu.VMEM((192, 128), F32),
             pltpu.VMEM((17, 8, 128), F32),
+            pltpu.VMEM((128, 128), F32),
+            pltpu.VMEM((NDEV, SLOTS, 128), F32),
             pltpu.VMEM((1536, 512), BF16),
             pltpu.VMEM((NDEV, SLOTS, 128), F32),
             pltpu.VMEM((NDEV, 4, 128), F32),
@@ -419,7 +456,7 @@
             dma((2,)), dma((2,)), dma, dma, dma, dma, dma, dma, dma, dma,
         ],
         compiler_params=pltpu.CompilerParams(collective_id=0, has_side_effects=True),
-    )(patch, block, template[0], science, variance, bad_pixels, across, vertical)[None]
+    )(patch.T, block.T, template[0], science, variance, bad_pixels, across, vertical)[None]
 
 
 def solution(mesh):

time: 103 us -> 96.7 us (0.939)
  Pallas kernels: 98.5 us -> 94.9 us
  local copies, waits for them, and re-layouts: 3.62 us -> 1.57 us
    pallas_call x1, Pallas kernels: 98.5 us -> 94.9 us  [body(): pl.pallas_call(kernel, out_shape=jax.ShapeDtypeStruct((32, 1024), F32), i...]
    unnamed x5 -> x1, local copies, waits for them, and re-layouts: 3.62 us -> 1.57 us
where the time goes in v3:
time: 96.7 us; the launch traced here: 96.5 us
  Pallas kernels  94.9 us (98%)
  local copies, waits for them, and re-layouts  1.57 us (2%)
    pallas_call x1, Pallas kernels, body(): pl.pallas_call(kernel, out_shape=jax.ShapeDtypeStruct((32, 1024), F32), i...  94.9 us

profile of v3, /device:TPU:24, one launch (start us, length us, event | category | flops | bytes accessed | tf_op | source)
XLA Modules:
  0.0 96.5 jit_solution(571978990524580437)
XLA Ops:
  0.0 94.9 %shard_map.82 = f32[32,1024]{1,0:T(8,128)} custom-call(s32[4,6]{1,0:T(4,128)} %bitcast.6, s32[4,6]{1,0:T(4,128)} %bitcast.7, bf16[32,1152]{1,0:T(8,128)(2,1)} %bitcast.5, bf16[6,4,32,128]{3,2,1,0:T(8,128)(2,1)} %science.1, bf16[6,4,32,128]{3,2,1,0:T(8,128)(2,1)} %variance.1, s32[6,4,32,128]{3,2,1,0:T(8,128)} %bad.1, bf16[256,512]{1,0:T(8,128)(2,1)} %constant.4.clone.across, ...), custom_call_target="tpu_custom_call" | custom-call | tf_op jit(solution)/shard_map/pallas_call | solution.py:427
  94.9 1.6 %copy.10 = f32[1,32,1024]{2,1,0:T(8,128)} copy(f32[1,32,1024]{2,1,0:T(8,128)} %bitcast.4) | data formatting | bytes 262144

commit v4 on v3

--- a/solution.py
+++ b/solution.py
@@ -53,23 +53,25 @@
 
 
 TILES = 9
-LEAD = 8
+LEAD = 7
 SLOTS = 24
 HALFWAY = (1, -1)
 Y_STEP = {0: 0, 1: 1, 2: 2, 3: -1}
 
 
 def kernel(
-    patch, block, strip, science, variance, bad, across, vertical, out,
+    patch, block, strip, science_in, variance_in, bad_in, across_in, vertical_in, out,
+    science, variance, bad, across, vertical,
     stage, got, packed, early, late, early_in, late_in, core, rim, smooth, images,
     sums, part, parts, rows, coef, codes, column, choose, spread, result, final,
-    local_sem, send_sem, ay, az, bz, by, halo_send, halo_recv, sum_send, sum_recv,
+    local_sem, input_sem, send_sem, ay, az, bz, by, halo_send, halo_recv, sum_send, sum_recv,
     early_send, early_recv, late_send, late_recv, final_send, final_recv,
 ):
     me = lax.axis_index("visit")
     tem = lax.axis_index("template")
     z, y = lax.div(me, NY), lax.rem(me, NY)
     visits = science.shape[0]
+    inputs = (science, variance, bad, across, vertical)
 
     def at(dz, dy):
         return (wrap(z + dz, NZ) * NY + wrap(y + dy, NY), tem)
@@ -102,6 +104,32 @@
                 local_sem,
             ).start()
 
+    sources = (science_in, variance_in, bad_in, across_in, vertical_in)
+    for k in range(5):
+        pltpu.make_async_copy(sources[k], inputs[k], input_sem.at[k]).start()
+    arrive(stage, local_sem)
+    pl.semaphore_wait(barrier, len(partners))
+
+    def slot(zz, yy):
+        return wrap(zz, NZ) * NY + wrap(yy, NY)
+
+    def a_ref(zz, yy):
+        return got.at[slot(zz, yy), pl.ds(0, LEAD)]
+
+    def b_ref(zz, yy):
+        return got.at[slot(zz, yy), pl.ds(LEAD, 2 * TILES - LEAD)]
+
+    a_own, b_own = stage.at[pl.ds(0, LEAD)], stage.at[pl.ds(LEAD, 2 * TILES - LEAD)]
+    for d in (1, 3, 2):
+        send(a_own, a_ref(z, y), send_sem, ay.at[d - 1], at(0, Y_STEP[d]))
+    for k, dz in enumerate(HALFWAY):
+        send(b_own, b_ref(z, y), send_sem, bz.at[k, 0], at(dz, 0))
+        send(a_own, a_ref(z, y), send_sem, az.at[k, 0, 0], at(dz, 0))
+    for k, dy in enumerate(HALFWAY):
+        send(b_own, b_ref(z, y), send_sem, by.at[k, 0], at(0, dy))
+    got[me] = stage[...]
+    for k in range(5):
+        arrive(inputs[k], input_sem.at[k])
     low = lax.broadcasted_iota(jnp.int32, (32, 128), 1) < 64
     lane = lax.broadcasted_iota(jnp.int32, (8, 128), 1)
 
@@ -124,28 +152,6 @@
                 pack(v * 4 + j, weigh(v, j), weigh(v + 3, j), 16)
     packed[pl.ds(12, NDEV, stride=16), :] = jnp.broadcast_to(targets[0:1], (NDEV, 128))
     early[...] = packed[...].reshape(NDEV, 16, 128).astype(BF16)
-
-    arrive(stage, local_sem)
-    pl.semaphore_wait(barrier, len(partners))
-
-    def slot(zz, yy):
-        return wrap(zz, NZ) * NY + wrap(yy, NY)
-
-    def a_ref(zz, yy):
-        return got.at[slot(zz, yy), pl.ds(0, LEAD)]
-
-    def b_ref(zz, yy):
-        return got.at[slot(zz, yy), pl.ds(LEAD, 2 * TILES - LEAD)]
-
-    a_own, b_own = stage.at[pl.ds(0, LEAD)], stage.at[pl.ds(LEAD, 2 * TILES - LEAD)]
-    for d in (1, 3, 2):
-        send(a_own, a_ref(z, y), send_sem, ay.at[d - 1], at(0, Y_STEP[d]))
-    for k, dz in enumerate(HALFWAY):
-        send(b_own, b_ref(z, y), send_sem, bz.at[k, 0], at(dz, 0))
-        send(a_own, a_ref(z, y), send_sem, az.at[k, 0, 0], at(dz, 0))
-    for k, dy in enumerate(HALFWAY):
-        send(b_own, b_ref(z, y), send_sem, by.at[k, 0], at(0, dy))
-    got[me] = stage[...]
     for d in (1, 3, 2):
         ref = a_ref(z, y - Y_STEP[d])
         arrive(ref, ay.at[d - 1])
@@ -160,7 +166,8 @@
         send(ref, ref, send_sem, by.at[2, index], at(0, dy))
 
     ring = NZ // 2
-    for s in range(1, ring + 1):
+
+    def z_first(s):
         for k, dz in enumerate(HALFWAY):
             if s == ring and k == 1:
                 continue
@@ -170,20 +177,31 @@
                 send(ref, ref, send_sem, bz.at[k, s], at(dz, 0))
             for q, dy in enumerate(HALFWAY):
                 send(ref, ref, send_sem, by.at[q, 2 * s - 1 + k], at(0, dy))
-        for d in (0, 1, 3, 2):
-            for k, dz in enumerate(HALFWAY):
-                if s == ring and k != (d >= 2):
-                    continue
-                ref = a_ref(z - dz * s, y - Y_STEP[d])
-                arrive(ref, az.at[k, s - 1, d])
-                if s < ring - 1 or (s == ring - 1 and k == (d >= 2)):
-                    send(ref, ref, send_sem, az.at[k, s, d], at(dz, 0))
-        if s == 1:
+
+    def y_first(s, d):
+        for k, dz in enumerate(HALFWAY):
+            if s == ring and k != (d >= 2):
+                continue
+            ref = a_ref(z - dz * s, y - Y_STEP[d])
+            arrive(ref, az.at[k, s - 1, d])
+            if s < ring - 1 or (s == ring - 1 and k == (d >= 2)):
+                send(ref, ref, send_sem, az.at[k, s, d], at(dz, 0))
+
+    def relays(s):
+        if s == 0:
             relay(z, 0)
-        else:
-            for k, dz in enumerate(HALFWAY):
-                relay(z - dz * (s - 1), 2 * (s - 1) - 1 + k)
-    relay(z - ring, NZ - 1)
+        for k, dz in enumerate(HALFWAY):
+            if s > 0 and 2 * s - 1 + k < NZ:
+                relay(z - dz * s, 2 * s - 1 + k)
+
+    due = {7 * (s - 1) // 2: s for s in range(1, ring + 1)}
+    for index in range(4 * ring):
+        if index in due:
+            z_first(due[index])
+            relays(due[index] - 1)
+        if index == 4 * ring - 4:
+            relays(ring)
+        y_first(index // 4 + 1, (0, 1, 3, 2)[index % 4])
     for index in range(NZ):
         s = (index + 1) // 2
         source = z - s if index % 2 == 1 else z + s
@@ -427,9 +445,14 @@
     return pl.pallas_call(
         kernel,
         out_shape=jax.ShapeDtypeStruct((32, 1024), F32),
-        in_specs=[smem, smem, anywhere] + [vmem] * 5,
+        in_specs=[smem, smem] + [anywhere] * 6,
         out_specs=vmem,
         scratch_shapes=[
+            pltpu.VMEM(science.shape, BF16),
+            pltpu.VMEM(variance.shape, BF16),
+            pltpu.VMEM(bad_pixels.shape, jnp.int32),
+            pltpu.VMEM(across.shape, BF16),
+            pltpu.VMEM(vertical.shape, BF16),
             pltpu.VMEM((18, 16, 128), BF16),
             pltpu.VMEM((NDEV, 18, 16, 128), BF16),
             pltpu.VMEM((1024, 128), F32),
@@ -452,7 +475,7 @@
             pltpu.VMEM((NDEV, SLOTS, 128), F32),
             pltpu.VMEM((NDEV, 4, 128), F32),
             pltpu.VMEM((NDEV, 4, 128), F32),
-            dma, dma, dma((3,)), dma((2, 8, 4)), dma((2, 8)), dma((3, NZ)),
+            dma, dma((5,)), dma, dma((3,)), dma((2, 8, 4)), dma((2, 8)), dma((3, NZ)),
             dma((2,)), dma((2,)), dma, dma, dma, dma, dma, dma, dma, dma,
         ],
         compiler_params=pltpu.CompilerParams(collective_id=0, has_side_effects=True),

time: 96.7 us -> 96.7 us (level); the launches traced: 96.5 us -> 94.9 us
  Pallas kernels: 94.9 us -> 93.4 us
    pallas_call x1, Pallas kernels: 94.9 us -> 93.4 us  [body(): pl.pallas_call(kernel, out_shape=jax.ShapeDtypeStruct((32, 1024), F32), i...]
where the time goes in v4:
time: 96.7 us; the launch traced here: 94.9 us
  Pallas kernels  93.4 us (97%)
  local copies, waits for them, and re-layouts  1.57 us (2%)
    pallas_call x1, Pallas kernels, body(): pl.pallas_call(kernel, out_shape=jax.ShapeDtypeStruct((32, 1024), F32), i...  93.4 us

profile of v4, /device:TPU:24, one launch (start us, length us, event | category | flops | bytes accessed | tf_op | source)
XLA Modules:
  0.0 94.9 jit_solution(12764248370853091441)
XLA Ops:
  0.0 93.4 %shard_map.82 = f32[32,1024]{1,0:T(8,128)} custom-call(s32[4,6]{1,0:T(4,128)} %bitcast.6, s32[4,6]{1,0:T(4,128)} %bitcast.7, bf16[32,1152]{1,0:T(8,128)(2,1)} %bitcast.5, bf16[6,4,32,128]{3,2,1,0:T(8,128)(2,1)} %science_in.1, bf16[6,4,32,128]{3,2,1,0:T(8,128)(2,1)} %variance_in.1, s32[6,4,32,128]{3,2,1,0:T(8,128)} %bad_in.1, ...), custom_call_target="tpu_custom_call" | custom-call | tf_op jit(solution)/shard_map/pallas_call | solution.py:445
  93.4 1.6 %copy.10 = f32[1,32,1024]{2,1,0:T(8,128)} copy(f32[1,32,1024]{2,1,0:T(8,128)} %bitcast.4) | data formatting | bytes 262144

commit v5 on v4

--- a/solution.py
+++ b/solution.py
@@ -53,7 +53,7 @@
 
 
 TILES = 9
-LEAD = 7
+LEAD = 9
 SLOTS = 24
 HALFWAY = (1, -1)
 Y_STEP = {0: 0, 1: 1, 2: 2, 3: -1}
@@ -224,60 +224,53 @@
         one(NDEV // 2)
         lax.fori_loop(1, NDEV // 2, two, 0)
 
-    for v in range(visits):
-        for j in range(4):
-            p, b = patch[j, v], block[j, v]
-            for h in range(2):
-                core[h, v * 4 + j, :, 0:128] = got[p, h * TILES + b]
-                core[h, v * 4 + j, :, 128:256] = got[p, h * TILES + b + 1]
-
-    def halo(source, dest, step, k):
+    def halo(half, source, dest, step, k):
         return pltpu.make_async_remote_copy(
-            src_ref=core.at[source], dst_ref=rim.at[dest],
-            send_sem=halo_send.at[k], recv_sem=halo_recv.at[k],
+            src_ref=core.at[half, source], dst_ref=rim.at[half, dest],
+            send_sem=halo_send.at[half, k], recv_sem=halo_recv.at[half, k],
             device_id=beside(step), device_id_type=MESH,
         )
 
-    down, up = halo(1, 0, 1, 0), halo(0, 1, -1, 1)
-
-    @pl.when(tem < NTEM - 1)
-    def _():
-        down.start()
-
-    @pl.when(tem > 0)
-    def _():
-        up.start()
-
-    def smear(piece, source):
+    downs = [halo(half, 1, 0, 1, 0) for half in range(2)]
+    ups = [halo(half, 0, 1, -1, 1) for half in range(2)]
+    for half in range(2):
+        for v in range(3):
+            for j in range(4):
+                p, b = patch[j, half * 3 + v], block[j, half * 3 + v]
+                for h in range(2):
+                    core[half, h, v * 4 + j, :, 0:128] = got[p, h * TILES + b]
+                    core[half, h, v * 4 + j, :, 128:256] = got[p, h * TILES + b + 1]
+
+        @pl.when(tem < NTEM - 1)
+        def _():
+            downs[half].start()
+
+        @pl.when(tem > 0)
+        def _():
+            ups[half].start()
+
+    def smear(half, piece, source):
         image = jnp.dot(
-            source.reshape(SLOTS * 16, 256), across[...], preferred_element_type=F32
+            source.reshape(12 * 16, 256), across[...], preferred_element_type=F32
         )
-        smooth[:, piece * 16 : piece * 16 + 16, :] = image.astype(BF16).reshape(SLOTS, 16, 512)
+        smooth[half * 12 : half * 12 + 12, piece * 16 : piece * 16 + 16, :] = image.astype(
+            BF16
+        ).reshape(12, 16, 512)
 
     push(early, early_in, early_send, early_recv)
     early_in[me] = early[me]
-    smear(1, core[0])
-    smear(2, core[1])
+    for half in range(2):
+        smear(half, 1, core[half, 0])
+        smear(half, 2, core[half, 1])
 
     @pl.when(tem == 0)
     def _():
-        rim[0] = jnp.zeros((SLOTS, 16, 256), BF16)
+        rim[:, 0] = jnp.zeros((2, 12, 16, 256), BF16)
 
     @pl.when(tem == NTEM - 1)
     def _():
-        rim[1] = jnp.zeros((SLOTS, 16, 256), BF16)
-
-    @pl.when(tem > 0)
-    def _():
-        down.wait_recv()
-
-    smear(0, rim[0])
-
-    @pl.when(tem < NTEM - 1)
-    def _():
-        up.wait_recv()
-
-    smear(3, rim[1])
+        rim[:, 1] = jnp.zeros((2, 12, 16, 256), BF16)
+
     row_id = lax.broadcasted_iota(jnp.int32, (144, 144), 0) & 7
     lane_id = lax.broadcasted_iota(jnp.int32, (144, 144), 1) & 7
     same_row = row_id == lane_id
@@ -315,7 +308,19 @@
         sums[v, 18:24, :] = jnp.zeros((6, 144), F32)
         return carry
 
-    lax.fori_loop(0, visits, gram, 0)
+    for half in range(2):
+
+        @pl.when(tem > 0)
+        def _():
+            downs[half].wait_recv()
+
+        @pl.when(tem < NTEM - 1)
+        def _():
+            ups[half].wait_recv()
+
+        smear(half, 0, rim[half, 0])
+        smear(half, 3, rim[half, 1])
+        lax.fori_loop(half * 3, half * 3 + 3, gram, 0)
     pick_row = lax.broadcasted_iota(jnp.int32, (144, 128), 0) >> 3
     pick_lane = lax.broadcasted_iota(jnp.int32, (144, 128), 1)
     dense = jnp.dot(
@@ -412,11 +417,11 @@
     )[0:64]
     ratio = numerator / scale
     both = jnp.concatenate([ratio[:, 0:256], ratio[:, 256:512]], axis=0).T
-    result[...] = both.reshape(NDEV, 4, 128)
+    result[...] = both.reshape(NDEV, 4, 128).astype(BF16)
     push(result, final, final_send, final_recv)
     final[me] = result[me]
     arrive(final.at[pl.ds(0, NDEV - 1)], final_recv)
-    whole = final[...]
+    whole = final[...].astype(F32)
     for m in range(4):
         left, right = whole[0:32, m, :], whole[32:64, m, :]
         out[:, m * 256 : m * 256 + 128] = jnp.where(low, left, pltpu.roll(right, 64, 1))
@@ -428,13 +433,15 @@
     arrive(late.at[pl.ds(0, NDEV - 1)], late_send)
     arrive(result.at[pl.ds(0, NDEV - 1)], final_send)
 
-    @pl.when(tem < NTEM - 1)
-    def _():
-        down.wait_send()
-
-    @pl.when(tem > 0)
-    def _():
-        up.wait_send()
+    for half in range(2):
+
+        @pl.when(tem < NTEM - 1)
+        def _():
+            downs[half].wait_send()
+
+        @pl.when(tem > 0)
+        def _():
+            ups[half].wait_send()
 
 
 def body(across, vertical, template, science, variance, bad_pixels, patch, block):
@@ -460,8 +467,8 @@
             pltpu.VMEM((NDEV, 12, 128), BF16),
             pltpu.VMEM((NDEV, 16, 128), BF16),
             pltpu.VMEM((NDEV, 12, 128), BF16),
-            pltpu.VMEM((2, SLOTS, 16, 256), BF16),
-            pltpu.VMEM((2, SLOTS, 16, 256), BF16),
+            pltpu.VMEM((2, 2, 12, 16, 256), BF16),
+            pltpu.VMEM((2, 2, 12, 16, 256), BF16),
             pltpu.VMEM((SLOTS, 64, 512), BF16),
             pltpu.VMEM((6, 128, 2048), BF16),
             pltpu.VMEM((6, 24, 144), F32),
@@ -473,10 +480,10 @@
             pltpu.VMEM((NDEV, SLOTS, 128), F32),
             pltpu.VMEM((1536, 512), BF16),
             pltpu.VMEM((NDEV, SLOTS, 128), F32),
-            pltpu.VMEM((NDEV, 4, 128), F32),
-            pltpu.VMEM((NDEV, 4, 128), F32),
+            pltpu.VMEM((NDEV, 4, 128), BF16),
+            pltpu.VMEM((NDEV, 4, 128), BF16),
             dma, dma((5,)), dma, dma((3,)), dma((2, 8, 4)), dma((2, 8)), dma((3, NZ)),
-            dma((2,)), dma((2,)), dma, dma, dma, dma, dma, dma, dma, dma,
+            dma((2, 2)), dma((2, 2)), dma, dma, dma, dma, dma, dma, dma, dma,
         ],
         compiler_params=pltpu.CompilerParams(collective_id=0, has_side_effects=True),
     )(patch.T, block.T, template[0], science, variance, bad_pixels, across, vertical)[None]

time: 96.7 us -> 96.3 us (level)
  no operation moved by 1% of the time
where the time goes in v5:
time: 96.3 us; the launch traced here: 94.8 us
  Pallas kernels  93.3 us (97%)
  local copies, waits for them, and re-layouts  1.57 us (2%)
    pallas_call x1, Pallas kernels, body(): pl.pallas_call(kernel, out_shape=jax.ShapeDtypeStruct((32, 1024), F32), i...  93.3 us

profile of v5, /device:TPU:24, one launch (start us, length us, event | category | flops | bytes accessed | tf_op | source)
XLA Modules:
  0.0 94.8 jit_solution(13314956599159322969)
XLA Ops:
  0.0 93.3 %shard_map.82 = f32[32,1024]{1,0:T(8,128)} custom-call(s32[4,6]{1,0:T(4,128)} %bitcast.6, s32[4,6]{1,0:T(4,128)} %bitcast.7, bf16[32,1152]{1,0:T(8,128)(2,1)} %bitcast.5, bf16[6,4,32,128]{3,2,1,0:T(8,128)(2,1)} %science_in.1, bf16[6,4,32,128]{3,2,1,0:T(8,128)(2,1)} %variance_in.1, s32[6,4,32,128]{3,2,1,0:T(8,128)} %bad_in.1, ...), custom_call_target="tpu_custom_call" | custom-call | tf_op jit(solution)/shard_map/pallas_call | solution.py:452
  93.3 1.6 %copy.10 = f32[1,32,1024]{2,1,0:T(8,128)} copy(f32[1,32,1024]{2,1,0:T(8,128)} %bitcast.4) | data formatting | bytes 262144

commit v6 on v5

--- a/solution.py
+++ b/solution.py
@@ -63,7 +63,7 @@
     patch, block, strip, science_in, variance_in, bad_in, across_in, vertical_in, out,
     science, variance, bad, across, vertical,
     stage, got, packed, early, late, early_in, late_in, core, rim, smooth, images,
-    sums, part, parts, rows, coef, codes, column, choose, spread, result, final,
+    sums, part, parts, rows, coef, codes, column, choose, result, final,
     local_sem, input_sem, send_sem, ay, az, bz, by, halo_send, halo_recv, sum_send, sum_recv,
     early_send, early_recv, late_send, late_recv, final_send, final_recv,
 ):
@@ -151,7 +151,7 @@
             if v < visits // 2:
                 pack(v * 4 + j, weigh(v, j), weigh(v + 3, j), 16)
     packed[pl.ds(12, NDEV, stride=16), :] = jnp.broadcast_to(targets[0:1], (NDEV, 128))
-    early[...] = packed[...].reshape(NDEV, 16, 128).astype(BF16)
+    early[...] = packed[...].reshape(NDEV, 4, 4, 128).astype(BF16)
     for d in (1, 3, 2):
         ref = a_ref(z, y - Y_STEP[d])
         arrive(ref, ay.at[d - 1])
@@ -378,50 +378,48 @@
         return carry
 
     lax.fori_loop(0, visits // 2, differ, 0)
-    for k in range(NDEV):
-        late[k] = packed[k * 12 : k * 12 + 12, :].astype(BF16)
+    late[...] = packed[0:768, :].reshape(NDEV, 3, 4, 128).astype(BF16)
     push(late, late_in, late_send, late_recv)
     late_in[me] = late[me]
 
     arrive(early_in.at[pl.ds(0, NDEV - 1)], early_recv)
     codes[...] = jnp.zeros((128, 128), F32)
     for k in range(NDEV):
-        value = early_in[k].astype(F32)
-        spread[k, 0:12, :] = value[0:12]
-        spread[k, 12:24, :] = pltpu.roll(value[0:12], 64, 1)
-        codes[k : k + 1, :] = value[12:13]
+        codes[k : k + 1, :] = early_in[k, 3].astype(F32)[0:1]
     across_codes = codes[...].T
-    for k in range(NDEV):
-        column[k] = jnp.broadcast_to(across_codes[0:SLOTS, k : k + 1], (SLOTS, 128))
-    code = column[...].reshape(NDEV * SLOTS, 128)
-    place = lax.broadcasted_iota(jnp.int32, (NDEV * SLOTS, 128), 1).astype(F32)
-    for q in range(4):
-        choose[:, q * 128 : q * 128 + 128] = jnp.where(
-            code == place + (q * 128.0 - 256.0), 1.0, 0.0
-        ).astype(BF16)
-    inner = (((0,), (0,)), ((), ()))
-    denominator = lax.dot_general(
-        spread[...].reshape(NDEV * SLOTS, 128).astype(BF16), choose[...], inner,
-        preferred_element_type=F32,
-    )[0:64]
+    place = lax.broadcasted_iota(jnp.int32, (NDEV * 12, 128), 1).astype(F32)
+    for p in range(2):
+        for k in range(NDEV):
+            column[p, k * 12 : k * 12 + 12, :] = jnp.broadcast_to(
+                across_codes[p * 12 : p * 12 + 12, k : k + 1], (12, 128)
+            )
+        code = column[p]
+        for q in range(4):
+            choose[p, :, q * 128 : q * 128 + 128] = jnp.where(
+                code == place + (q * 128.0 - 256.0), 1.0, 0.0
+            ).astype(BF16)
+
+    def collect(box):
+        values = box.astype(F32).reshape(NDEV * 12, 128).astype(BF16)
+        inner = (((0,), (0,)), ((), ()))
+        sums = [
+            lax.dot_general(values, choose[p], inner, preferred_element_type=F32)
+            for p in range(2)
+        ]
+        return sums[0][0:64] + sums[1][64:128]
+
+    denominator = collect(early_in[:, 0:3])
     scale = jnp.sqrt(jnp.maximum(denominator, 1.0))
 
     arrive(late_in.at[pl.ds(0, NDEV - 1)], late_recv)
-    for k in range(NDEV):
-        value = late_in[k].astype(F32)
-        spread[k, 0:12, :] = value
-        spread[k, 12:24, :] = pltpu.roll(value, 64, 1)
-    numerator = lax.dot_general(
-        spread[...].reshape(NDEV * SLOTS, 128).astype(BF16), choose[...], inner,
-        preferred_element_type=F32,
-    )[0:64]
+    numerator = collect(late_in[...])
     ratio = numerator / scale
     both = jnp.concatenate([ratio[:, 0:256], ratio[:, 256:512]], axis=0).T
-    result[...] = both.reshape(NDEV, 4, 128).astype(BF16)
+    result[...] = both.reshape(NDEV, 4, 128)
     push(result, final, final_send, final_recv)
     final[me] = result[me]
     arrive(final.at[pl.ds(0, NDEV - 1)], final_recv)
-    whole = final[...].astype(F32)
+    whole = final[...]
     for m in range(4):
         left, right = whole[0:32, m, :], whole[32:64, m, :]
         out[:, m * 256 : m * 256 + 128] = jnp.where(low, left, pltpu.roll(right, 64, 1))
@@ -463,10 +461,10 @@
             pltpu.VMEM((18, 16, 128), BF16),
             pltpu.VMEM((NDEV, 18, 16, 128), BF16),
             pltpu.VMEM((1024, 128), F32),
-            pltpu.VMEM((NDEV, 16, 128), BF16),
-            pltpu.VMEM((NDEV, 12, 128), BF16),
-            pltpu.VMEM((NDEV, 16, 128), BF16),
-            pltpu.VMEM((NDEV, 12, 128), BF16),
+            pltpu.VMEM((NDEV, 4, 4, 128), BF16),
+            pltpu.VMEM((NDEV, 3, 4, 128), BF16),
+            pltpu.VMEM((NDEV, 4, 4, 128), BF16),
+            pltpu.VMEM((NDEV, 3, 4, 128), BF16),
             pltpu.VMEM((2, 2, 12, 16, 256), BF16),
             pltpu.VMEM((2, 2, 12, 16, 256), BF16),
             pltpu.VMEM((SLOTS, 64, 512), BF16),
@@ -477,11 +475,10 @@
             pltpu.VMEM((192, 128), F32),
             pltpu.VMEM((17, 8, 128), F32),
             pltpu.VMEM((128, 128), F32),
-            pltpu.VMEM((NDEV, SLOTS, 128), F32),
-            pltpu.VMEM((1536, 512), BF16),
-            pltpu.VMEM((NDEV, SLOTS, 128), F32),
-            pltpu.VMEM((NDEV, 4, 128), BF16),
-            pltpu.VMEM((NDEV, 4, 128), BF16),
+            pltpu.VMEM((2, NDEV * 12, 128), F32),
+            pltpu.VMEM((2, NDEV * 12, 512), BF16),
+            pltpu.VMEM((NDEV, 4, 128), F32),
+            pltpu.VMEM((NDEV, 4, 128), F32),
             dma, dma((5,)), dma, dma((3,)), dma((2, 8, 4)), dma((2, 8)), dma((3, NZ)),
             dma((2, 2)), dma((2, 2)), dma, dma, dma, dma, dma, dma, dma, dma,
         ],

time: 96.3 us -> 94.3 us (0.979)
  Pallas kernels: 93.3 us -> 92.2 us
    pallas_call x1, Pallas kernels: 93.3 us -> 92.2 us  [body(): pl.pallas_call(kernel, out_shape=jax.ShapeDtypeStruct((32, 1024), F32), i...]
where the time goes in v6:
time: 94.3 us; the launch traced here: 93.7 us
  Pallas kernels  92.2 us (98%)
  local copies, waits for them, and re-layouts  1.57 us (2%)
    pallas_call x1, Pallas kernels, body(): pl.pallas_call(kernel, out_shape=jax.ShapeDtypeStruct((32, 1024), F32), i...  92.2 us

profile of v6, /device:TPU:24, one launch (start us, length us, event | category | flops | bytes accessed | tf_op | source)
XLA Modules:
  0.0 93.7 jit_solution(6523683955921032842)
XLA Ops:
  0.0 92.2 %shard_map.82 = f32[32,1024]{1,0:T(8,128)} custom-call(s32[4,6]{1,0:T(4,128)} %bitcast.6, s32[4,6]{1,0:T(4,128)} %bitcast.7, bf16[32,1152]{1,0:T(8,128)(2,1)} %bitcast.5, bf16[6,4,32,128]{3,2,1,0:T(8,128)(2,1)} %science_in.1, bf16[6,4,32,128]{3,2,1,0:T(8,128)(2,1)} %variance_in.1, s32[6,4,32,128]{3,2,1,0:T(8,128)} %bad_in.1, ...), custom_call_target="tpu_custom_call" | custom-call | tf_op jit(solution)/shard_map/pallas_call | solution.py:450
  92.2 1.6 %copy.10 = f32[1,32,1024]{2,1,0:T(8,128)} copy(f32[1,32,1024]{2,1,0:T(8,128)} %bitcast.4) | data formatting | bytes 262144

commit v7 on v6

--- a/solution.py
+++ b/solution.py
@@ -128,6 +128,56 @@
     for k, dy in enumerate(HALFWAY):
         send(b_own, b_ref(z, y), send_sem, by.at[k, 0], at(0, dy))
     got[me] = stage[...]
+    for d in (1, 3, 2):
+        ref = a_ref(z, y - Y_STEP[d])
+        arrive(ref, ay.at[d - 1])
+        for k, dz in enumerate(HALFWAY):
+            send(ref, ref, send_sem, az.at[k, 0, d], at(dz, 0))
+
+    def relay(source, index):
+        k = index % 2
+        dy = HALFWAY[k]
+        ref = b_ref(source, y - dy)
+        arrive(ref, by.at[k, index])
+        send(ref, ref, send_sem, by.at[2, index], at(0, dy))
+
+    ring = NZ // 2
+
+    def z_first(s):
+        for k, dz in enumerate(HALFWAY):
+            if s == ring and k == 1:
+                continue
+            ref = b_ref(z - dz * s, y)
+            arrive(ref, bz.at[k, s - 1])
+            if s < ring - k:
+                send(ref, ref, send_sem, bz.at[k, s], at(dz, 0))
+            for q, dy in enumerate(HALFWAY):
+                send(ref, ref, send_sem, by.at[q, 2 * s - 1 + k], at(0, dy))
+
+    def y_first(s, d):
+        for k, dz in enumerate(HALFWAY):
+            if s == ring and k != (d >= 2):
+                continue
+            ref = a_ref(z - dz * s, y - Y_STEP[d])
+            arrive(ref, az.at[k, s - 1, d])
+            if s < ring - 1 or (s == ring - 1 and k == (d >= 2)):
+                send(ref, ref, send_sem, az.at[k, s, d], at(dz, 0))
+
+    def relays(s):
+        if s == 0:
+            relay(z, 0)
+        for k, dz in enumerate(HALFWAY):
+            if s > 0 and 2 * s - 1 + k < NZ:
+                relay(z - dz * s, 2 * s - 1 + k)
+
+    due = {7 * (s - 1) // 2: s for s in range(1, ring + 1)}
+    for index in range(4 * ring - 4):
+        if index in due:
+            z_first(due[index])
+            relays(due[index] - 1)
+        y_first(index // 4 + 1, (0, 1, 3, 2)[index % 4])
+    relays(ring)
+
     for k in range(5):
         arrive(inputs[k], input_sem.at[k])
     low = lax.broadcasted_iota(jnp.int32, (32, 128), 1) < 64
@@ -152,56 +202,9 @@
                 pack(v * 4 + j, weigh(v, j), weigh(v + 3, j), 16)
     packed[pl.ds(12, NDEV, stride=16), :] = jnp.broadcast_to(targets[0:1], (NDEV, 128))
     early[...] = packed[...].reshape(NDEV, 4, 4, 128).astype(BF16)
-    for d in (1, 3, 2):
-        ref = a_ref(z, y - Y_STEP[d])
-        arrive(ref, ay.at[d - 1])
-        for k, dz in enumerate(HALFWAY):
-            send(ref, ref, send_sem, az.at[k, 0, d], at(dz, 0))
-
-    def relay(source, index):
-        k = index % 2
-        dy = HALFWAY[k]
-        ref = b_ref(source, y - dy)
-        arrive(ref, by.at[k, index])
-        send(ref, ref, send_sem, by.at[2, index], at(0, dy))
-
-    ring = NZ // 2
-
-    def z_first(s):
-        for k, dz in enumerate(HALFWAY):
-            if s == ring and k == 1:
-                continue
-            ref = b_ref(z - dz * s, y)
-            arrive(ref, bz.at[k, s - 1])
-            if s < ring - k:
-                send(ref, ref, send_sem, bz.at[k, s], at(dz, 0))
-            for q, dy in enumerate(HALFWAY):
-                send(ref, ref, send_sem, by.at[q, 2 * s - 1 + k], at(0, dy))
-
-    def y_first(s, d):
-        for k, dz in enumerate(HALFWAY):
-            if s == ring and k != (d >= 2):
-                continue
-            ref = a_ref(z - dz * s, y - Y_STEP[d])
-            arrive(ref, az.at[k, s - 1, d])
-            if s < ring - 1 or (s == ring - 1 and k == (d >= 2)):
-                send(ref, ref, send_sem, az.at[k, s, d], at(dz, 0))
-
-    def relays(s):
-        if s == 0:
-            relay(z, 0)
-        for k, dz in enumerate(HALFWAY):
-            if s > 0 and 2 * s - 1 + k < NZ:
-                relay(z - dz * s, 2 * s - 1 + k)
-
-    due = {7 * (s - 1) // 2: s for s in range(1, ring + 1)}
-    for index in range(4 * ring):
-        if index in due:
-            z_first(due[index])
-            relays(due[index] - 1)
-        if index == 4 * ring - 4:
-            relays(ring)
-        y_first(index // 4 + 1, (0, 1, 3, 2)[index % 4])
+
+    for d in (0, 1, 3, 2):
+        y_first(ring, d)
     for index in range(NZ):
         s = (index + 1) // 2
         source = z - s if index % 2 == 1 else z + s

time: 94.3 us -> 94.3 us (level)
  no operation moved by 1% of the time
where the time goes in v7:
time: 94.3 us; the launch traced here: 93.7 us
  Pallas kernels  92.2 us (98%)
  local copies, waits for them, and re-layouts  1.57 us (2%)
    pallas_call x1, Pallas kernels, body(): pl.pallas_call(kernel, out_shape=jax.ShapeDtypeStruct((32, 1024), F32), i...  92.2 us

profile of v7, /device:TPU:24, one launch (start us, length us, event | category | flops | bytes accessed | tf_op | source)
XLA Modules:
  0.0 93.7 jit_solution(5705433007352987538)
XLA Ops:
  0.0 92.2 %shard_map.82 = f32[32,1024]{1,0:T(8,128)} custom-call(s32[4,6]{1,0:T(4,128)} %bitcast.6, s32[4,6]{1,0:T(4,128)} %bitcast.7, bf16[32,1152]{1,0:T(8,128)(2,1)} %bitcast.5, bf16[6,4,32,128]{3,2,1,0:T(8,128)(2,1)} %science_in.1, bf16[6,4,32,128]{3,2,1,0:T(8,128)(2,1)} %variance_in.1, s32[6,4,32,128]{3,2,1,0:T(8,128)} %bad_in.1, ...), custom_call_target="tpu_custom_call" | custom-call | tf_op jit(solution)/shard_map/pallas_call | solution.py:453
  92.2 1.6 %copy.10 = f32[1,32,1024]{2,1,0:T(8,128)} copy(f32[1,32,1024]{2,1,0:T(8,128)} %bitcast.4) | data formatting | bytes 262144
